TPU v7x, 256 devices: a whole 4x4x8 slice. The times are simulated.
256 devices in a mesh: space: 32 (over x, z), rep: 8 (over y, core).
Axes of the slice: x: 4, y: 4, z: 8, core: 2. Of those that a mesh axis runs over, the one named last changes fastest.
Arguments:
- feats: bfloat16 [8, 128, 64, 512], P('rep', 'space'), may hold values from -6 to 6
- cotangent: bfloat16 [8, 128, 64, 512], P('rep', 'space'), may hold values from -6 to 6
- weight: bfloat16 [27, 64, 64], replicated, may hold values from -0.15625 to 0.15625
- bias: float32 [64], replicated, may hold values from -3 to 3
- neighbours: int32 [8, 128, 26], P('rep', 'space'), may hold values from -1 to 127, as said below
- occupancy: int32 [8, 128, 512], P('rep', 'space'), may hold values from 0 to 1, as said below
Outputs:
- out_feats: bfloat16 [8, 128, 64, 512], P('rep', 'space')
- in_grad: bfloat16 [8, 128, 64, 512], P('rep', 'space')
- weight_grad: float32 [27, 64, 64], replicated
- bias_grad: float32 [64], replicated
Inputs may be any that keep to these rules, and one draw needn't show every extreme that they name: Slot s of a district lies on space index s // 4. On each space index the live bricks fill the first slots; a live brick has at least one occupied voxel and a dead slot none. A brick of a district lies in the slab of its space index at one of 8 x 8 positions; neighbours[s, j] is the slot of the live brick adjacent in direction j, which lies on space index s // 4 + dx; dead slots list only -1, and the lists are symmetric. In every district some space index holds 4 live bricks. `occupancy`: dead slots are all zero.
All inputs are finite; a program needn't handle non-finite values.
Results may differ from a plain program's by a relative error of at most 0.0085.
Values may be sent and summed in bfloat16 or wider, within the bound.
A program may use at most 128 MiB of HBM per device.

v0:
```python
import functools
import math

import jax
import jax.numpy as jnp
from jax import lax
from jax.experimental import pallas as pl
from jax.experimental.pallas import tpu as pltpu
from jax.sharding import PartitionSpec as P

INTERPRET = False

DIRECTIONS = [
    (a, b, c) for a in (-1, 0, 1) for b in (-1, 0, 1) for c in (-1, 0, 1) if (a, b, c) != (0, 0, 0)
]
OFFSETS = [(a - 1, b - 1, c - 1) for a in range(3) for b in range(3) for c in range(3)]
STRIDES = (64, 8, 1)
ZERO_SLOT = 12


def offset_terms(shift):
    moving = [axis for axis in range(3) if shift[axis] != 0]
    terms = []
    for pick in range(1 << len(moving)):
        out_axes = [axis for n, axis in enumerate(moving) if (pick >> n) & 1]
        direction = tuple(shift[axis] if axis in out_axes else 0 for axis in range(3))
        flat = sum(STRIDES[axis] * (shift[axis] - (8 * shift[axis] if axis in out_axes else 0)) for axis in range(3))
        pattern = [(axis, shift[axis], axis in out_axes) for axis in moving]
        terms.append((direction, (-flat) % 512, pattern))
    return terms


def gather_columns(src_ref, tbl_ref, brick, col_ref, sign, edges):
    base = brick * 26
    for k, off in enumerate(OFFSETS):
        shift = tuple(sign * s for s in off)
        val = None
        for direction, roll, pattern in offset_terms(shift):
            if direction == (0, 0, 0):
                field = src_ref[brick].astype(jnp.float32)
            else:
                slot = tbl_ref[base + DIRECTIONS.index(direction)]
                field = src_ref[slot].astype(jnp.float32)
            if roll:
                field = pltpu.roll(field, roll, 1)
            if val is None:
                val = field
                continue
            mask = None
            for axis, step, out in pattern:
                m = edges[(axis, step)] if out else jnp.logical_not(edges[(axis, step)])
                mask = m if mask is None else jnp.logical_and(mask, m)
            val = jnp.where(mask, field, val)
        col_ref[pl.ds(k * 64, 64), :] = val.astype(jnp.bfloat16)


def edge_masks(shape):
    v = lax.broadcasted_iota(jnp.int32, shape, 1)
    coords = (v >> 6, (v >> 3) & 7, v & 7)
    edges = {}
    for axis in range(3):
        edges[(axis, -1)] = coords[axis] == 0
        edges[(axis, 1)] = coords[axis] == 7
    return edges


def forward_kernel(tbl_ref, x_ref, cot_ref, occ_ref, w_ref, bias_ref, out_ref, gp_ref, dw_ref, db_ref, col_ref):
    slots, channels, voxels = cot_ref.shape
    edges = edge_masks((channels, voxels))
    dw_ref[...] = jnp.zeros_like(dw_ref)
    db_ref[...] = jnp.zeros_like(db_ref)

    def brick_step(brick, carry):
        gather_columns(x_ref, tbl_ref, brick, col_ref, 1, edges)
        pre = jnp.dot(w_ref[...], col_ref[...], preferred_element_type=jnp.float32) + bias_ref[...]
        sig = 1.0 / (1.0 + jnp.exp(-pre))
        keep = occ_ref[brick]
        masked = x_ref[brick].astype(jnp.float32)
        out_ref[brick] = (masked + keep * pre * sig).astype(out_ref.dtype)
        gp = (cot_ref[brick].astype(jnp.float32) * keep * sig * (1.0 + pre * (1.0 - sig))).astype(jnp.bfloat16)
        gp_ref[brick] = gp
        dw_ref[...] += lax.dot_general(
            gp, col_ref[...], (((1,), (1,)), ((), ())), preferred_element_type=jnp.float32
        )
        db_ref[...] += jnp.sum(gp.astype(jnp.float32), axis=1, keepdims=True)
        return carry

    lax.fori_loop(0, slots, brick_step, 0)


def backward_kernel(tbl_ref, g_ref, cot_ref, occ_ref, wt_ref, in_grad_ref, col_ref):
    slots, channels, voxels = cot_ref.shape
    edges = edge_masks((channels, voxels))

    def brick_step(brick, carry):
        gather_columns(g_ref, tbl_ref, brick, col_ref, -1, edges)
        back = jnp.dot(wt_ref[...], col_ref[...], preferred_element_type=jnp.float32)
        keep = occ_ref[brick]
        in_grad_ref[brick] = (keep * (cot_ref[brick].astype(jnp.float32) + back)).astype(in_grad_ref.dtype)
        return carry

    lax.fori_loop(0, slots, brick_step, 0)


def vmem_specs(n):
    return [pl.BlockSpec(memory_space=pltpu.VMEM)] * n


def run_forward(tbl, table, cot, occ, w_all, bias):
    slots, channels, voxels = cot.shape
    return pl.pallas_call(
        forward_kernel,
        out_shape=(
            jax.ShapeDtypeStruct((slots, channels, voxels), jnp.bfloat16),
            jax.ShapeDtypeStruct((slots, channels, voxels), jnp.bfloat16),
            jax.ShapeDtypeStruct((channels, 27 * channels), jnp.float32),
            jax.ShapeDtypeStruct((channels, 1), jnp.float32),
        ),
        in_specs=[pl.BlockSpec(memory_space=pltpu.SMEM)] + vmem_specs(5),
        out_specs=tuple(vmem_specs(4)),
        scratch_shapes=[pltpu.VMEM((27 * channels, voxels), jnp.bfloat16)],
        interpret=INTERPRET,
    )(tbl, table, cot, occ, w_all, bias)


def run_backward(tbl, table, cot, occ, w_t):
    slots, channels, voxels = cot.shape
    return pl.pallas_call(
        backward_kernel,
        out_shape=jax.ShapeDtypeStruct((slots, channels, voxels), jnp.bfloat16),
        in_specs=[pl.BlockSpec(memory_space=pltpu.SMEM)] + vmem_specs(4),
        out_specs=pl.BlockSpec(memory_space=pltpu.VMEM),
        scratch_shapes=[pltpu.VMEM((27 * channels, voxels), jnp.bfloat16)],
        interpret=INTERPRET,
    )(tbl, table, cot, occ, w_t)


def exchange_planes(field):
    size = lax.axis_size("space")
    up = [(i, i + 1) for i in range(size - 1)]
    down = [(i + 1, i) for i in range(size - 1)]
    voxels = field.shape[-1]
    low = field[:, :, :64]
    high = field[:, :, voxels - 64 :]
    from_left = lax.ppermute(high, "space", up)
    from_right = lax.ppermute(low, "space", down)
    left = jnp.pad(from_left, ((0, 0), (0, 0), (voxels - 64, 0)))
    right = jnp.pad(from_right, ((0, 0), (0, 0), (0, voxels - 64)))
    zero = jnp.zeros((1,) + field.shape[1:], field.dtype)
    return jnp.concatenate([field, left, right, zero])


def slot_table(neighbour_ids, my_index):
    slots = neighbour_ids.shape[0]
    dx = jnp.array([d[0] for d in DIRECTIONS], jnp.int32)[None, :]
    local = neighbour_ids - (my_index + dx) * slots
    base = jnp.where(dx == 0, 0, jnp.where(dx < 0, slots, 2 * slots))
    table = jnp.where(neighbour_ids >= 0, base + jnp.clip(local, 0, slots - 1), 3 * slots)
    return table.reshape(-1).astype(jnp.int32)


SUM_AXES = ("space", "rep")


def all_sum(weight_terms, bias_terms):
    flat = jnp.concatenate([weight_terms.reshape(-1), bias_terms])
    count = lax.axis_size(SUM_AXES)
    rep_size = lax.axis_size("rep")
    me = lax.axis_index("space") * rep_size + lax.axis_index("rep")
    bits = [b for b in (0, 1, 3, 6, 2, 4, 7, 5) if (1 << b) < count]
    whole = flat.shape[0]
    padded = -(-whole // count) * count
    x = jnp.pad(flat, (0, padded - whole))
    for b in bits:
        bit = (me >> b) & 1
        halves = x.reshape(2, -1)
        keep = jnp.where(bit == 0, halves[0], halves[1])
        send = jnp.where(bit == 0, halves[1], halves[0])
        pairs = [(i, i ^ (1 << b)) for i in range(count)]
        x = keep + lax.ppermute(send, SUM_AXES, pairs)
    for b in reversed(bits):
        bit = (me >> b) & 1
        pairs = [(i, i ^ (1 << b)) for i in range(count)]
        other = lax.ppermute(x, SUM_AXES, pairs)
        x = jnp.where(bit == 0, jnp.concatenate([x, other]), jnp.concatenate([other, x]))
    x = x[:whole]
    return x[: weight_terms.size].reshape(weight_terms.shape), x[weight_terms.size :]


def on_device(feats, cotangent, weight, bias, neighbours, occupancy):
    filled = occupancy[0]
    incoming = cotangent[0]
    slot_count, channels = (feats.shape[1], feats.shape[2])
    my_index = lax.axis_index("space")
    masked = feats[0] * filled.astype(jnp.bfloat16)[:, None, :]
    keep_float = filled.astype(jnp.float32)[:, None, :]
    tbl = slot_table(neighbours[0], my_index)
    w_all = weight.transpose(1, 0, 2).reshape(channels, 27 * channels)
    w_t = weight.transpose(2, 0, 1).reshape(channels, 27 * channels)
    result, grad_pre, dw, db = run_forward(
        tbl, exchange_planes(masked), incoming, keep_float, w_all, bias.reshape(channels, 1)
    )
    in_grad = run_backward(tbl, exchange_planes(grad_pre), incoming, keep_float, w_t)
    weight_terms = dw.reshape(channels, 27, channels).transpose(1, 0, 2)
    weight_total, bias_total = all_sum(weight_terms, db.reshape(channels))
    normaliser = 1.0 / math.sqrt(
        feats.shape[0] * lax.axis_size("rep") * slot_count * lax.axis_size("space") * 512
    )
    return (result[None], in_grad[None], weight_total * normaliser, bias_total * normaliser)


def solution(mesh):
    placed = (
        P("rep", "space", None, None),
        P("rep", "space", None, None),
        P(),
        P(),
        P("rep", "space", None),
        P("rep", "space", None),
    )
    return jax.shard_map(
        on_device,
        mesh=mesh,
        in_specs=placed,
        out_specs=(P("rep", "space", None, None), P("rep", "space", None, None), P(), P()),
        check_vma=False,
    )
```

profile of v0, /device:TPU:6, one launch (start us, length us, event | category | flops | bytes accessed | tf_op | source)
XLA Modules:
  0.0 137.4 jit_solution(8748142635923013203)
XLA Ops:
  0.6 0.8 fusion.15
  1.4 1.0 bitcast_multiply_fusion
  2.4 0.1 fusion.14
  2.5 3.8 %collective-permute-start = (bf16[4,64,64]{2,1,0:T(8,128)(2,1)S(1)}, bf16[4,64,64]{2,1,0:T(8,128)(2,1)S(1)}, u32[]{:S(2)}, u32[]{:S(2)}) collective-permute-start(bf16[4,64,64]{2,1,0:T(8,128)(2,1)S(1)} %get-tuple-element.14), channel_id=1, source_target_pairs={{0,8},{8,16},{16,24},{24,32},{32,40},{40,48},{48,56},{56,64},{64,7... | collective-permute-start | bytes 98312 | tf_op jit(solution)/shard_map/ppermute | solution.py:145
  6.3 6.1 %collective-permute-start.1 = (bf16[4,64,64]{2,1,0:T(8,128)(2,1)S(1)}, bf16[4,64,64]{2,1,0:T(8,128)(2,1)S(1)}, u32[]{:S(2)}, u32[]{:S(2)}) collective-permute-start(bf16[4,64,64]{2,1,0:T(8,128)(2,1)S(1)} %get-tuple-element.15), channel_id=1, source_target_pairs={{8,0},{16,8},{24,16},{32,24},{40,32},{48,40},{56,48},{64,56},{72,6... | collective-permute-start | bytes 98312 | tf_op jit(solution)/shard_map/ppermute | solution.py:146
  12.5 0.8 squeeze.6
  13.2 0.7 add_multiply_fusion
  14.0 0.7 add.55
  14.7 0.5 compare_select_fusion.tbl_ref
  15.2 0.6 copy.23
  15.8 1.4 copy.17.bias_ref
  17.2 0.3 copy.16
  17.5 1.1 reshape.98.w_ref
  18.7 1.1 fusion.8.x_ref
  19.7 16.4 %shard_map.102 = (bf16[4,64,512]{2,1,0:T(8,128)(2,1)}, bf16[4,64,512]{2,1,0:T(8,128)(2,1)}, f32[64,1728]{1,0:T(8,128)}, f32[64,1]{1,0:T(8,128)}) custom-call(s32[104]{0:T(128)} %compare_select_fusion.tbl_ref, bf16[13,64,512]{2,1,0:T(8,128)(2,1)} %fusion.8.x_ref, bf16[4,64,512]{2,1,0:T(8,128)(2,1)} %bitcast.20, f32[4,1,512]{2,1,0:T(1,128)} %bitcast.23, ...), custom_call_target="tpu_custom_call" | custom-call | tf_op jit(solution)/shard_map/pallas_call | solution.py:111
  36.1 1.4 %reshape.101 = f32[64,27,64]{2,1,0:T(8,128)S(1)} reshape(f32[64,1728]{1,0:T(8,128)} %get-tuple-element.10) | data formatting | bytes 884736 | tf_op jit(solution)/shard_map/reshape | solution.py:204
  37.6 0.5 copy.19
  38.1 0.2 reshape.102
  38.3 0.6 copy-done.2
  38.9 0.1 reduce
  39.0 0.1 collective-permute-start.4
  39.1 1.5 %collective-permute-done.4 = f32[55424]{0:T(1024)S(1)} collective-permute-done((f32[55424]{0:T(1024)S(1)}, f32[55424]{0:T(1024)S(1)}, u32[]{:S(2)}, u32[]{:S(2)}) %collective-permute-start.4) | collective-permute-done | bytes 221728 | tf_op jit(solution)/shard_map/ppermute | solution.py:180
  40.6 0.1 slice_select_fusion.1
  40.7 1.7 %collective-permute-start.5 = (f32[27712]{0:T(1024)S(1)}, f32[27712]{0:T(1024)S(1)}, u32[]{:S(2)}, u32[]{:S(2)}) collective-permute-start(f32[27712]{0:T(1024)S(1)} %slice_select_fusion.1), channel_id=1, source_target_pairs={{0,2},{1,3},{2,0},{3,1},{4,6},{5,7},{6,4},{7,5},{8,10},{9,11},{10,... | collective-permute-start | bytes 332552 | tf_op jit(solution)/shard_map/ppermute | solution.py:180
  42.4 3.6 %collective-permute-done.5 = f32[27712]{0:T(1024)S(1)} collective-permute-done((f32[27712]{0:T(1024)S(1)}, f32[27712]{0:T(1024)S(1)}, u32[]{:S(2)}, u32[]{:S(2)}) %collective-permute-start.5) | collective-permute-done | bytes 110880 | tf_op jit(solution)/shard_map/ppermute | solution.py:180
  46.0 0.1 select_add_fusion.1
  46.2 0.1 collective-permute-start.6
  46.3 4.2 %collective-permute-done.6 = f32[13856]{0:T(1024)S(1)} collective-permute-done((f32[13856]{0:T(1024)S(1)}, f32[13856]{0:T(1024)S(1)}, u32[]{:S(2)}, u32[]{:S(2)}) %collective-permute-start.6) | collective-permute-done | bytes 55456 | tf_op jit(solution)/shard_map/ppermute | solution.py:180
  50.5 0.1 select_add_fusion.2
  50.6 0.6 collective-permute-start.7
  51.2 3.3 %collective-permute-done.7 = f32[6928]{0:T(1024)S(1)} collective-permute-done((f32[6928]{0:T(1024)S(1)}, f32[6928]{0:T(1024)S(1)}, u32[]{:S(2)}, u32[]{:S(2)}) %collective-permute-start.7) | collective-permute-done | bytes 27744 | tf_op jit(solution)/shard_map/ppermute | solution.py:180
  54.7 3.2 %collective-permute-start.8 = (f32[3464]{0:T(1024)S(1)}, f32[3464]{0:T(1024)S(1)}, u32[]{:S(2)}, u32[]{:S(2)}) collective-permute-start(f32[3464]{0:T(1024)S(1)} %slice_select_fusion.4), channel_id=1, source_target_pairs={{0,4},{1,5},{2,6},{3,7},{4,0},{5,1},{6,2},{7,3},{8,12},{9,13},{10,... | collective-permute-start | bytes 41576 | tf_op jit(solution)/shard_map/ppermute | solution.py:180
  57.9 2.0 %collective-permute-done.8 = f32[3464]{0:T(1024)S(1)} collective-permute-done((f32[3464]{0:T(1024)S(1)}, f32[3464]{0:T(1024)S(1)}, u32[]{:S(2)}, u32[]{:S(2)}) %collective-permute-start.8) | collective-permute-done | bytes 13888 | tf_op jit(solution)/shard_map/ppermute | solution.py:180
  60.1 0.2 collective-permute-start.9
  60.3 4.4 %collective-permute-done.9 = f32[1732]{0:T(1024)S(1)} collective-permute-done((f32[1732]{0:T(1024)S(1)}, f32[1732]{0:T(1024)S(1)}, u32[]{:S(2)}, u32[]{:S(2)}) %collective-permute-start.9) | collective-permute-done | bytes 6960 | tf_op jit(solution)/shard_map/ppermute | solution.py:180
  64.9 1.1 collective-permute-start.10
  66.0 4.0 %collective-permute-done.10 = f32[866]{0:T(1024)S(1)} collective-permute-done((f32[866]{0:T(1024)S(1)}, f32[866]{0:T(1024)S(1)}, u32[]{:S(2)}, u32[]{:S(2)}) %collective-permute-start.10) | collective-permute-done | bytes 3496 | tf_op jit(solution)/shard_map/ppermute | solution.py:180
  70.1 4.3 %collective-permute-start.11 = (f32[433]{0:T(512)S(1)}, f32[433]{0:T(512)S(1)}, u32[]{:S(2)}, u32[]{:S(2)}) collective-permute-start(f32[433]{0:T(512)S(1)} %slice_select_fusion.7), channel_id=1, source_target_pairs={{0,32},{1,33},{2,34},{3,35},{4,36},{5,37},{6,38},{7,39},{8,40},{9,... | collective-permute-start | bytes 5204 | tf_op jit(solution)/shard_map/ppermute | solution.py:180
  74.4 3.2 %collective-permute-done.11 = f32[433]{0:T(512)S(1)} collective-permute-done((f32[433]{0:T(512)S(1)}, f32[433]{0:T(512)S(1)}, u32[]{:S(2)}, u32[]{:S(2)}) %collective-permute-start.11) | collective-permute-done | bytes 1764 | tf_op jit(solution)/shard_map/ppermute | solution.py:180
  77.7 4.3 %collective-permute-start.12 = (f32[433]{0:T(512)S(1)}, f32[433]{0:T(512)S(1)}, u32[]{:S(2)}, u32[]{:S(2)}) collective-permute-start(f32[433]{0:T(512)S(1)} %select_add_fusion.7), channel_id=1, source_target_pairs={{0,32},{1,33},{2,34},{3,35},{4,36},{5,37},{6,38},{7,39},{8,40},{9,... | collective-permute-start | bytes 5204 | tf_op jit(solution)/shard_map/ppermute | solution.py:184
  82.0 3.2 %collective-permute-done.12 = f32[433]{0:T(512)S(1)} collective-permute-done((f32[433]{0:T(512)S(1)}, f32[433]{0:T(512)S(1)}, u32[]{:S(2)}, u32[]{:S(2)}) %collective-permute-start.12) | collective-permute-done | bytes 1764 | tf_op jit(solution)/shard_map/ppermute | solution.py:184
  85.3 1.1 collective-permute-start.13
  86.4 4.0 %collective-permute-done.13 = f32[866]{0:T(1024)S(1)} collective-permute-done((f32[866]{0:T(1024)S(1)}, f32[866]{0:T(1024)S(1)}, u32[]{:S(2)}, u32[]{:S(2)}) %collective-permute-start.13) | collective-permute-done | bytes 3496 | tf_op jit(solution)/shard_map/ppermute | solution.py:184
  90.5 0.4 collective-permute-start.14
  90.9 4.4 %collective-permute-done.14 = f32[1732]{0:T(1024)S(1)} collective-permute-done((f32[1732]{0:T(1024)S(1)}, f32[1732]{0:T(1024)S(1)}, u32[]{:S(2)}, u32[]{:S(2)}) %collective-permute-start.14) | collective-permute-done | bytes 6960 | tf_op jit(solution)/shard_map/ppermute | solution.py:184
  95.4 3.2 %collective-permute-start.15 = (f32[3464]{0:T(1024)S(1)}, f32[3464]{0:T(1024)S(1)}, u32[]{:S(2)}, u32[]{:S(2)}) collective-permute-start(f32[3464]{0:T(1024)S(1)} %maximum_select_fusion.5), channel_id=1, source_target_pairs={{0,4},{1,5},{2,6},{3,7},{4,0},{5,1},{6,2},{7,3},{8,12},{9,13},{10,... | collective-permute-start | bytes 41576 | tf_op jit(solution)/shard_map/ppermute | solution.py:184
  98.5 2.2 %collective-permute-done.15 = f32[3464]{0:T(1024)S(1)} collective-permute-done((f32[3464]{0:T(1024)S(1)}, f32[3464]{0:T(1024)S(1)}, u32[]{:S(2)}, u32[]{:S(2)}) %collective-permute-start.15) | collective-permute-done | bytes 13888 | tf_op jit(solution)/shard_map/ppermute | solution.py:184
  100.8 0.6 collective-permute-start.16
  101.4 3.3 %collective-permute-done.16 = f32[6928]{0:T(1024)S(1)} collective-permute-done((f32[6928]{0:T(1024)S(1)}, f32[6928]{0:T(1024)S(1)}, u32[]{:S(2)}, u32[]{:S(2)}) %collective-permute-start.16) | collective-permute-done | bytes 27744 | tf_op jit(solution)/shard_map/ppermute | solution.py:184
  104.8 0.1 collective-permute-start.17
  104.9 0.9 copy.20.wt_ref
  105.8 3.3 %collective-permute-done.17 = f32[13856]{0:T(1024)S(1)} collective-permute-done((f32[13856]{0:T(1024)S(1)}, f32[13856]{0:T(1024)S(1)}, u32[]{:S(2)}, u32[]{:S(2)}) %collective-permute-start.17) | collective-permute-done | bytes 55456 | tf_op jit(solution)/shard_map/ppermute | solution.py:184
  109.1 0.1 maximum_select_fusion.2
  109.2 1.5 %collective-permute-start.18 = (f32[27712]{0:T(1024)S(1)}, f32[27712]{0:T(1024)S(1)}, u32[]{:S(2)}, u32[]{:S(2)}) collective-permute-start(f32[27712]{0:T(1024)S(1)} %maximum_select_fusion.2), channel_id=1, source_target_pairs={{0,2},{1,3},{2,0},{3,1},{4,6},{5,7},{6,4},{7,5},{8,10},{9,11},{10,... | collective-permute-start | bytes 332552 | tf_op jit(solution)/shard_map/ppermute | solution.py:184
  110.7 0.1 fusion.13
  110.8 2.0 %collective-permute-start.2 = (bf16[4,64,64]{2,1,0:T(8,128)(2,1)S(1)}, bf16[4,64,64]{2,1,0:T(8,128)(2,1)S(1)}, u32[]{:S(2)}, u32[]{:S(2)}) collective-permute-start(bf16[4,64,64]{2,1,0:T(8,128)(2,1)S(1)} %get-tuple-element.12), channel_id=1, source_target_pairs={{0,8},{8,16},{16,24},{24,32},{32,40},{40,48},{48,56},{56,64},{64,7... | collective-permute-start | bytes 98312 | tf_op jit(solution)/shard_map/ppermute | solution.py:145
  112.8 6.0 %collective-permute-start.3 = (bf16[4,64,64]{2,1,0:T(8,128)(2,1)S(1)}, bf16[4,64,64]{2,1,0:T(8,128)(2,1)S(1)}, u32[]{:S(2)}, u32[]{:S(2)}) collective-permute-start(bf16[4,64,64]{2,1,0:T(8,128)(2,1)S(1)} %get-tuple-element.13), channel_id=1, source_target_pairs={{8,0},{16,8},{24,16},{32,24},{40,32},{48,40},{56,48},{64,56},{72,6... | collective-permute-start | bytes 98312 | tf_op jit(solution)/shard_map/ppermute | solution.py:146
  118.8 0.1 maximum_select_fusion.1
  118.9 0.1 collective-permute-start.19
  119.1 1.6 %collective-permute-done.3 = bf16[4,64,64]{2,1,0:T(8,128)(2,1)S(1)} collective-permute-done((bf16[4,64,64]{2,1,0:T(8,128)(2,1)S(1)}, bf16[4,64,64]{2,1,0:T(8,128)(2,1)S(1)}, u32[]{:S(2)}, u32[]{:S(2)}) %collective-permute-start.3) | collective-permute-done | bytes 32800 | tf_op jit(solution)/shard_map/ppermute | solution.py:146
  120.7 1.1 fusion.11.g_ref
  121.7 13.9 %shard_map.103 = bf16[4,64,512]{2,1,0:T(8,128)(2,1)} custom-call(s32[104]{0:T(128)} %compare_select_fusion.tbl_ref, bf16[13,64,512]{2,1,0:T(8,128)(2,1)} %fusion.11.g_ref, bf16[4,64,512]{2,1,0:T(8,128)(2,1)} %bitcast.21, f32[4,1,512]{2,1,0:T(1,128)} %bitcast.24, bf16[64,1728]{1,0:T(8,128)(2,1)} %copy.20.wt_ref), custom_call_target="tpu_custom_call" | custom-call | tf_op jit(solution)/shard_map/pallas_call | solution.py:128
  135.7 0.5 slice_multiply_fusion.1
  136.3 1.1 mul.36
  (34 shorter events, 1.7 us)
Async XLA Ops:
  0.6 16.6 %copy-start = (bf16[27,64,64]{2,1,0:T(8,128)(2,1)S(1)}, bf16[27,64,64]{2,1,0:T(8,128)(2,1)}, u32[]{:S(2)}) copy-start(bf16[27,64,64]{2,1,0:T(8,128)(2,1)} %param.9) | copy-start | bytes 663556
  2.5 16.2 %collective-permute-start = (bf16[4,64,64]{2,1,0:T(8,128)(2,1)S(1)}, bf16[4,64,64]{2,1,0:T(8,128)(2,1)S(1)}, u32[]{:S(2)}, u32[]{:S(2)}) collective-permute-start(bf16[4,64,64]{2,1,0:T(8,128)(2,1)S(1)} %get-tuple-element.14), channel_id=1, source_target_pairs={{0,8},{8,16},{16,24},{24,32},{32,40},{40,48},{48,56},{56,64},{64,7... | collective-permute-start | bytes 98312 | tf_op jit(solution)/shard_map/ppermute | solution.py:145
  6.3 12.4 %collective-permute-start.1 = (bf16[4,64,64]{2,1,0:T(8,128)(2,1)S(1)}, bf16[4,64,64]{2,1,0:T(8,128)(2,1)S(1)}, u32[]{:S(2)}, u32[]{:S(2)}) collective-permute-start(bf16[4,64,64]{2,1,0:T(8,128)(2,1)S(1)} %get-tuple-element.15), channel_id=1, source_target_pairs={{8,0},{16,8},{24,16},{32,24},{40,32},{48,40},{56,48},{64,56},{72,6... | collective-permute-start | bytes 98312 | tf_op jit(solution)/shard_map/ppermute | solution.py:146
  38.1 0.8 copy-start.2
  39.0 1.6 %collective-permute-start.4 = (f32[55424]{0:T(1024)S(1)}, f32[55424]{0:T(1024)S(1)}, u32[]{:S(2)}, u32[]{:S(2)}) collective-permute-start(f32[55424]{0:T(1024)S(1)} %slice_select_fusion), channel_id=1, source_target_pairs={{0,1},{1,0},{2,3},{3,2},{4,5},{5,4},{6,7},{7,6},{8,9},{9,8},{10,11... | collective-permute-start | bytes 665096 | tf_op jit(solution)/shard_map/ppermute | solution.py:180
  40.7 5.3 %collective-permute-start.5 = (f32[27712]{0:T(1024)S(1)}, f32[27712]{0:T(1024)S(1)}, u32[]{:S(2)}, u32[]{:S(2)}) collective-permute-start(f32[27712]{0:T(1024)S(1)} %slice_select_fusion.1), channel_id=1, source_target_pairs={{0,2},{1,3},{2,0},{3,1},{4,6},{5,7},{6,4},{7,5},{8,10},{9,11},{10,... | collective-permute-start | bytes 332552 | tf_op jit(solution)/shard_map/ppermute | solution.py:180
  46.1 64.6 %copy-start.1 = (bf16[4,64,512]{2,1,0:T(8,128)(2,1)S(1)}, bf16[4,64,512]{2,1,0:T(8,128)(2,1)}, u32[]{:S(2)}) copy-start(bf16[4,64,512]{2,1,0:T(8,128)(2,1)} %get-tuple-element.9) | copy-start | bytes 786436
  46.2 4.3 %collective-permute-start.6 = (f32[13856]{0:T(1024)S(1)}, f32[13856]{0:T(1024)S(1)}, u32[]{:S(2)}, u32[]{:S(2)}) collective-permute-start(f32[13856]{0:T(1024)S(1)} %slice_select_fusion.2), channel_id=1, source_target_pairs={{0,8},{1,9},{2,10},{3,11},{4,12},{5,13},{6,14},{7,15},{8,0},{9,1},... | collective-permute-start | bytes 166280 | tf_op jit(solution)/shard_map/ppermute | solution.py:180
  50.6 3.9 %collective-permute-start.7 = (f32[6928]{0:T(1024)S(1)}, f32[6928]{0:T(1024)S(1)}, u32[]{:S(2)}, u32[]{:S(2)}) collective-permute-start(f32[6928]{0:T(1024)S(1)} %slice_select_fusion.3), channel_id=1, source_target_pairs={{0,64},{1,65},{2,66},{3,67},{4,68},{5,69},{6,70},{7,71},{8,72},{9,... | collective-permute-start | bytes 83144 | tf_op jit(solution)/shard_map/ppermute | solution.py:180
  54.7 5.3 %collective-permute-start.8 = (f32[3464]{0:T(1024)S(1)}, f32[3464]{0:T(1024)S(1)}, u32[]{:S(2)}, u32[]{:S(2)}) collective-permute-start(f32[3464]{0:T(1024)S(1)} %slice_select_fusion.4), channel_id=1, source_target_pairs={{0,4},{1,5},{2,6},{3,7},{4,0},{5,1},{6,2},{7,3},{8,12},{9,13},{10,... | collective-permute-start | bytes 41576 | tf_op jit(solution)/shard_map/ppermute | solution.py:180
  60.1 4.6 %collective-permute-start.9 = (f32[1732]{0:T(1024)S(1)}, f32[1732]{0:T(1024)S(1)}, u32[]{:S(2)}, u32[]{:S(2)}) collective-permute-start(f32[1732]{0:T(1024)S(1)} %slice_select_fusion.5), channel_id=1, source_target_pairs={{0,16},{1,17},{2,18},{3,19},{4,20},{5,21},{6,22},{7,23},{8,24},{9,... | collective-permute-start | bytes 20792 | tf_op jit(solution)/shard_map/ppermute | solution.py:180
  64.9 5.1 %collective-permute-start.10 = (f32[866]{0:T(1024)S(1)}, f32[866]{0:T(1024)S(1)}, u32[]{:S(2)}, u32[]{:S(2)}) collective-permute-start(f32[866]{0:T(1024)S(1)} %slice_select_fusion.6), channel_id=1, source_target_pairs={{0,128},{1,129},{2,130},{3,131},{4,132},{5,133},{6,134},{7,135},{8... | collective-permute-start | bytes 10400 | tf_op jit(solution)/shard_map/ppermute | solution.py:180
  70.1 7.5 %collective-permute-start.11 = (f32[433]{0:T(512)S(1)}, f32[433]{0:T(512)S(1)}, u32[]{:S(2)}, u32[]{:S(2)}) collective-permute-start(f32[433]{0:T(512)S(1)} %slice_select_fusion.7), channel_id=1, source_target_pairs={{0,32},{1,33},{2,34},{3,35},{4,36},{5,37},{6,38},{7,39},{8,40},{9,... | collective-permute-start | bytes 5204 | tf_op jit(solution)/shard_map/ppermute | solution.py:180
  77.7 7.5 %collective-permute-start.12 = (f32[433]{0:T(512)S(1)}, f32[433]{0:T(512)S(1)}, u32[]{:S(2)}, u32[]{:S(2)}) collective-permute-start(f32[433]{0:T(512)S(1)} %select_add_fusion.7), channel_id=1, source_target_pairs={{0,32},{1,33},{2,34},{3,35},{4,36},{5,37},{6,38},{7,39},{8,40},{9,... | collective-permute-start | bytes 5204 | tf_op jit(solution)/shard_map/ppermute | solution.py:184
  85.3 5.1 %collective-permute-start.13 = (f32[866]{0:T(1024)S(1)}, f32[866]{0:T(1024)S(1)}, u32[]{:S(2)}, u32[]{:S(2)}) collective-permute-start(f32[866]{0:T(1024)S(1)} %maximum_select_fusion.7), channel_id=1, source_target_pairs={{0,128},{1,129},{2,130},{3,131},{4,132},{5,133},{6,134},{7,135},{8... | collective-permute-start | bytes 10400 | tf_op jit(solution)/shard_map/ppermute | solution.py:184
  90.5 4.8 %collective-permute-start.14 = (f32[1732]{0:T(1024)S(1)}, f32[1732]{0:T(1024)S(1)}, u32[]{:S(2)}, u32[]{:S(2)}) collective-permute-start(f32[1732]{0:T(1024)S(1)} %maximum_select_fusion.6), channel_id=1, source_target_pairs={{0,16},{1,17},{2,18},{3,19},{4,20},{5,21},{6,22},{7,23},{8,24},{9,... | collective-permute-start | bytes 20792 | tf_op jit(solution)/shard_map/ppermute | solution.py:184
  95.4 5.3 %collective-permute-start.15 = (f32[3464]{0:T(1024)S(1)}, f32[3464]{0:T(1024)S(1)}, u32[]{:S(2)}, u32[]{:S(2)}) collective-permute-start(f32[3464]{0:T(1024)S(1)} %maximum_select_fusion.5), channel_id=1, source_target_pairs={{0,4},{1,5},{2,6},{3,7},{4,0},{5,1},{6,2},{7,3},{8,12},{9,13},{10,... | collective-permute-start | bytes 41576 | tf_op jit(solution)/shard_map/ppermute | solution.py:184
  100.8 3.9 %collective-permute-start.16 = (f32[6928]{0:T(1024)S(1)}, f32[6928]{0:T(1024)S(1)}, u32[]{:S(2)}, u32[]{:S(2)}) collective-permute-start(f32[6928]{0:T(1024)S(1)} %maximum_select_fusion.4), channel_id=1, source_target_pairs={{0,64},{1,65},{2,66},{3,67},{4,68},{5,69},{6,70},{7,71},{8,72},{9,... | collective-permute-start | bytes 83144 | tf_op jit(solution)/shard_map/ppermute | solution.py:184
  104.8 4.3 %collective-permute-start.17 = (f32[13856]{0:T(1024)S(1)}, f32[13856]{0:T(1024)S(1)}, u32[]{:S(2)}, u32[]{:S(2)}) collective-permute-start(f32[13856]{0:T(1024)S(1)} %maximum_select_fusion.3), channel_id=1, source_target_pairs={{0,8},{1,9},{2,10},{3,11},{4,12},{5,13},{6,14},{7,15},{8,0},{9,1},... | collective-permute-start | bytes 166280 | tf_op jit(solution)/shard_map/ppermute | solution.py:184
  109.2 9.6 %collective-permute-start.18 = (f32[27712]{0:T(1024)S(1)}, f32[27712]{0:T(1024)S(1)}, u32[]{:S(2)}, u32[]{:S(2)}) collective-permute-start(f32[27712]{0:T(1024)S(1)} %maximum_select_fusion.2), channel_id=1, source_target_pairs={{0,2},{1,3},{2,0},{3,1},{4,6},{5,7},{6,4},{7,5},{8,10},{9,11},{10,... | collective-permute-start | bytes 332552 | tf_op jit(solution)/shard_map/ppermute | solution.py:184
  110.8 8.3 %collective-permute-start.2 = (bf16[4,64,64]{2,1,0:T(8,128)(2,1)S(1)}, bf16[4,64,64]{2,1,0:T(8,128)(2,1)S(1)}, u32[]{:S(2)}, u32[]{:S(2)}) collective-permute-start(bf16[4,64,64]{2,1,0:T(8,128)(2,1)S(1)} %get-tuple-element.12), channel_id=1, source_target_pairs={{0,8},{8,16},{16,24},{24,32},{32,40},{40,48},{48,56},{56,64},{64,7... | collective-permute-start | bytes 98312 | tf_op jit(solution)/shard_map/ppermute | solution.py:145
  112.8 7.8 %collective-permute-start.3 = (bf16[4,64,64]{2,1,0:T(8,128)(2,1)S(1)}, bf16[4,64,64]{2,1,0:T(8,128)(2,1)S(1)}, u32[]{:S(2)}, u32[]{:S(2)}) collective-permute-start(bf16[4,64,64]{2,1,0:T(8,128)(2,1)S(1)} %get-tuple-element.13), channel_id=1, source_target_pairs={{8,0},{16,8},{24,16},{32,24},{40,32},{48,40},{56,48},{64,56},{72,6... | collective-permute-start | bytes 98312 | tf_op jit(solution)/shard_map/ppermute | solution.py:146
  118.9 16.7 %collective-permute-start.19 = (f32[55424]{0:T(1024)S(1)}, f32[55424]{0:T(1024)S(1)}, u32[]{:S(2)}, u32[]{:S(2)}) collective-permute-start(f32[55424]{0:T(1024)S(1)} %maximum_select_fusion.1), channel_id=1, source_target_pairs={{0,1},{1,0},{2,3},{3,2},{4,5},{5,4},{6,7},{7,6},{8,9},{9,8},{10,11... | collective-permute-start | bytes 665096 | tf_op jit(solution)/shard_map/ppermute | solution.py:184
where the time goes:
time: 138 us; the launch traced here: 137 us
  waiting for transfers between devices  48.2 us (35%)
  starting transfers between devices  40.5 us (29%)
  Pallas kernels  30.3 us (22%)
  local copies, waits for them, and re-layouts  9.93 us (7%)
  other arithmetic  7.55 us (5%)
    ppermute x8, waiting for transfers between devices, all_sum(): x = keep + lax.ppermute(send, SUM_AXES, pairs)  26.2 us
    ppermute x8, waiting for transfers between devices, all_sum(): other = lax.ppermute(x, SUM_AXES, pairs)  20.4 us
    pallas_call x1, Pallas kernels, run_forward(): pl.pallas_call(forward_kernel, out_shape=(jax.ShapeDtypeStruct((slots, ch...  16.4 us
    pallas_call x1, Pallas kernels, run_backward(): pl.pallas_call(backward_kernel, out_shape=jax.ShapeDtypeStruct((slots, ch...  13.9 us
    ppermute x2, starting transfers between devices, exchange_planes(): from_right = lax.ppermute(low, 'space', down)  12.1 us
    ppermute x8, starting transfers between devices, all_sum(): other = lax.ppermute(x, SUM_AXES, pairs)  11.3 us
    ppermute x8, starting transfers between devices, all_sum(): x = keep + lax.ppermute(send, SUM_AXES, pairs)  11.3 us
    ppermute x2, starting transfers between devices, exchange_planes(): from_left = lax.ppermute(high, 'space', up)  5.82 us
  transfers between devices with their start and end apart: 20, of which 16 were waited for; matrix products, arithmetic and copies ran while one was open for 6% of the time, Pallas kernels for 10%

commit v1 on v0

--- a/solution.py
+++ b/solution.py
@@ -9,6 +9,7 @@
 from jax.sharding import PartitionSpec as P
 
 INTERPRET = False
+REMOTE_INTERPRET = False
 
 DIRECTIONS = [
     (a, b, c) for a in (-1, 0, 1) for b in (-1, 0, 1) for c in (-1, 0, 1) if (a, b, c) != (0, 0, 0)
@@ -160,30 +161,105 @@
 
 
 SUM_AXES = ("space", "rep")
+SUM_ORDER = (0, 1, 3, 6, 2, 4, 7, 5)
+
+
+def partner_of(me, bit, rep_size):
+    own = (me // (1 << bit)) % 2
+    other = me + (1 - 2 * own) * (1 << bit)
+    return own, (other // rep_size, other % rep_size)
+
+
+def reduce_kernel(bits, rep_size, x_ref, o_ref, buf, recv, full, send_sem, recv_sem, local_sem):
+    rows = buf.shape[0]
+    me = lax.axis_index("space") * rep_size + lax.axis_index("rep")
+    mesh_ids = pl.DeviceIdType.MESH
+    barrier = pltpu.get_barrier_semaphore()
+    for bit in bits:
+        pl.semaphore_signal(barrier, 1, device_id=partner_of(me, bit, rep_size)[1], device_id_type=mesh_ids)
+    pl.semaphore_wait(barrier, len(bits))
+    first = pltpu.make_async_copy(x_ref, buf, local_sem)
+    first.start()
+    first.wait()
+    lo = 0
+    length = rows
+    for step, bit in enumerate(bits[:-1]):
+        own, device = partner_of(me, bit, rep_size)
+        half = length // 2
+        keep_lo = pl.multiple_of(lo + own * half, 8)
+        send_lo = pl.multiple_of(lo + (1 - own) * half, 8)
+        at = rows - (rows >> step)
+        copy = pltpu.make_async_remote_copy(
+            src_ref=buf.at[pl.ds(send_lo, half)],
+            dst_ref=recv.at[pl.ds(at, half)],
+            send_sem=send_sem.at[step],
+            recv_sem=recv_sem.at[step],
+            device_id=device,
+            device_id_type=mesh_ids,
+        )
+        copy.start()
+        copy.wait()
+        buf[pl.ds(keep_lo, half)] += recv[pl.ds(at, half)]
+        lo = keep_lo
+        length = half
+    last = len(bits) - 1
+    own, device = partner_of(me, bits[last], rep_size)
+    at = rows - length
+    copy = pltpu.make_async_remote_copy(
+        src_ref=buf.at[pl.ds(lo, length)],
+        dst_ref=recv.at[pl.ds(at, length)],
+        send_sem=send_sem.at[last],
+        recv_sem=recv_sem.at[last],
+        device_id=device,
+        device_id_type=mesh_ids,
+    )
+    copy.start()
+    copy.wait()
+    full[pl.ds(lo, length)] = buf[pl.ds(lo, length)] + recv[pl.ds(at, length)]
+    for step in reversed(range(last)):
+        own, device = partner_of(me, bits[step], rep_size)
+        copy = pltpu.make_async_remote_copy(
+            src_ref=full.at[pl.ds(lo, length)],
+            dst_ref=full.at[pl.ds(lo, length)],
+            send_sem=send_sem.at[last + 1 + step],
+            recv_sem=recv_sem.at[last + 1 + step],
+            device_id=device,
+            device_id_type=mesh_ids,
+        )
+        copy.start()
+        copy.wait()
+        lo = pl.multiple_of(lo - own * length, 8)
+        length = 2 * length
+    o_ref[...] = full[...]
 
 
 def all_sum(weight_terms, bias_terms):
     flat = jnp.concatenate([weight_terms.reshape(-1), bias_terms])
     count = lax.axis_size(SUM_AXES)
     rep_size = lax.axis_size("rep")
-    me = lax.axis_index("space") * rep_size + lax.axis_index("rep")
-    bits = [b for b in (0, 1, 3, 6, 2, 4, 7, 5) if (1 << b) < count]
+    bits = tuple(b for b in SUM_ORDER if (1 << b) < count)
+    unit = 8 << (len(bits) - 1)
     whole = flat.shape[0]
-    padded = -(-whole // count) * count
-    x = jnp.pad(flat, (0, padded - whole))
-    for b in bits:
-        bit = (me >> b) & 1
-        halves = x.reshape(2, -1)
-        keep = jnp.where(bit == 0, halves[0], halves[1])
-        send = jnp.where(bit == 0, halves[1], halves[0])
-        pairs = [(i, i ^ (1 << b)) for i in range(count)]
-        x = keep + lax.ppermute(send, SUM_AXES, pairs)
-    for b in reversed(bits):
-        bit = (me >> b) & 1
-        pairs = [(i, i ^ (1 << b)) for i in range(count)]
-        other = lax.ppermute(x, SUM_AXES, pairs)
-        x = jnp.where(bit == 0, jnp.concatenate([x, other]), jnp.concatenate([other, x]))
-    x = x[:whole]
+    rows = -(-(-(-whole // 128)) // unit) * unit
+    x = jnp.pad(flat, (0, rows * 128 - whole)).reshape(rows, 128)
+    steps = 2 * len(bits) - 1
+    summed = pl.pallas_call(
+        functools.partial(reduce_kernel, bits, rep_size),
+        out_shape=jax.ShapeDtypeStruct((rows, 128), jnp.float32),
+        in_specs=[pl.BlockSpec(memory_space=pltpu.VMEM)],
+        out_specs=pl.BlockSpec(memory_space=pltpu.VMEM),
+        scratch_shapes=[
+            pltpu.VMEM((rows, 128), jnp.float32),
+            pltpu.VMEM((rows, 128), jnp.float32),
+            pltpu.VMEM((rows, 128), jnp.float32),
+            pltpu.SemaphoreType.DMA((steps,)),
+            pltpu.SemaphoreType.DMA((steps,)),
+            pltpu.SemaphoreType.DMA(()),
+        ],
+        compiler_params=pltpu.CompilerParams(collective_id=0, has_side_effects=True),
+        interpret=REMOTE_INTERPRET,
+    )(x)
+    x = summed.reshape(-1)[:whole]
     return x[: weight_terms.size].reshape(weight_terms.shape), x[weight_terms.size :]
 
 

time: 138 us -> 124 us (0.90)
  the two profiles are of different devices: /device:TPU:6 before, /device:TPU:1 now
where the time goes in v1:
time: 124 us
  Pallas kernels  92.6 us (75%)
  starting transfers between devices  11.1 us (9%)
  local copies, waits for them, and re-layouts  10.8 us (9%)
  other arithmetic  8.27 us (7%)
    pallas_call x1, Pallas kernels, all_sum(): pl.pallas_call(functools.partial(reduce_kernel, bits, rep_size), out_shap...  62.3 us
    pallas_call x1, Pallas kernels, run_forward(): pl.pallas_call(forward_kernel, out_shape=(jax.ShapeDtypeStruct((slots, ch...  16.4 us
    pallas_call x1, Pallas kernels, run_backward(): pl.pallas_call(backward_kernel, out_shape=jax.ShapeDtypeStruct((slots, ch...  13.9 us
    ppermute x2, starting transfers between devices, exchange_planes(): from_left = lax.ppermute(high, 'space', up)  8.55 us
    ppermute x2, starting transfers between devices, exchange_planes(): from_right = lax.ppermute(low, 'space', down)  2.58 us
  transfers between devices with their start and end apart: 4, of which 0 were waited for; matrix products, arithmetic and copies ran while one was open for 11% of the time, Pallas kernels for 50%

profile of v1, /device:TPU:1, one launch (start us, length us, event | category | flops | bytes accessed | tf_op | source)
XLA Modules:
  0.0 123.6 jit_solution(10225154718499520545)
XLA Ops:
  0.6 0.0 copy-start
  0.6 0.8 fusion.15
  1.4 1.0 bitcast_multiply_fusion
  2.4 0.1 fusion.14
  2.5 4.4 %collective-permute-start = (bf16[4,64,64]{2,1,0:T(8,128)(2,1)S(1)}, bf16[4,64,64]{2,1,0:T(8,128)(2,1)S(1)}, u32[]{:S(2)}, u32[]{:S(2)}) collective-permute-start(bf16[4,64,64]{2,1,0:T(8,128)(2,1)S(1)} %get-tuple-element.14), channel_id=1, source_target_pairs={{0,8},{8,16},{16,24},{24,32},{32,40},{40,48},{48,56},{56,64},{64,7... | collective-permute-start | bytes 98312 | tf_op jit(solution)/shard_map/ppermute | solution.py:146
  6.9 1.3 %collective-permute-start.1 = (bf16[4,64,64]{2,1,0:T(8,128)(2,1)S(1)}, bf16[4,64,64]{2,1,0:T(8,128)(2,1)S(1)}, u32[]{:S(2)}, u32[]{:S(2)}) collective-permute-start(bf16[4,64,64]{2,1,0:T(8,128)(2,1)S(1)} %get-tuple-element.15), channel_id=1, source_target_pairs={{8,0},{16,8},{24,16},{32,24},{40,32},{48,40},{56,48},{64,56},{72,6... | collective-permute-start | bytes 98312 | tf_op jit(solution)/shard_map/ppermute | solution.py:147
  8.2 0.8 squeeze.10
  8.9 0.7 add_multiply_fusion
  9.6 0.1 sub.12
  9.7 0.7 add.28
  10.3 0.1 add.29
  10.4 0.5 compare_select_fusion.tbl_ref
  10.9 0.6 copy.23
  11.5 1.4 %copy.17.bias_ref = f32[64,1]{1,0:T(8,128)} copy(f32[64,1]{0,1:T(1,128)} %bitcast.29) | data formatting | bytes 512 | tf_op jit(solution)/shard_map/reshape | solution.py:277
  12.9 0.0 copy-done
  12.9 0.9 copy.20.wt_ref
  13.8 0.3 copy.16
  14.1 1.1 reshape.67.w_ref
  15.2 0.1 pad.32.clone
  15.3 0.0 collective-permute-done
  15.3 0.0 collective-permute-done.1
  15.3 1.1 fusion.8.x_ref
  16.3 16.4 %shard_map.102 = (bf16[4,64,512]{2,1,0:T(8,128)(2,1)}, bf16[4,64,512]{2,1,0:T(8,128)(2,1)}, f32[64,1728]{1,0:T(8,128)}, f32[64,1]{1,0:T(8,128)}) custom-call(s32[104]{0:T(128)} %compare_select_fusion.tbl_ref, bf16[13,64,512]{2,1,0:T(8,128)(2,1)} %fusion.8.x_ref, bf16[4,64,512]{2,1,0:T(8,128)(2,1)} %bitcast.24, f32[4,1,512]{2,1,0:T(1,128)} %bitcast.27, ...), custom_call_target="tpu_custom_call" | custom-call | tf_op jit(solution)/shard_map/pallas_call | solution.py:112
  32.7 1.0 fusion.13
  33.7 4.2 %collective-permute-start.2 = (bf16[4,64,64]{2,1,0:T(8,128)(2,1)S(1)}, bf16[4,64,64]{2,1,0:T(8,128)(2,1)S(1)}, u32[]{:S(2)}, u32[]{:S(2)}) collective-permute-start(bf16[4,64,64]{2,1,0:T(8,128)(2,1)S(1)} %get-tuple-element.12), channel_id=1, source_target_pairs={{0,8},{8,16},{16,24},{24,32},{32,40},{40,48},{48,56},{56,64},{64,7... | collective-permute-start | bytes 98312 | tf_op jit(solution)/shard_map/ppermute | solution.py:146
  37.9 1.3 %collective-permute-start.3 = (bf16[4,64,64]{2,1,0:T(8,128)(2,1)S(1)}, bf16[4,64,64]{2,1,0:T(8,128)(2,1)S(1)}, u32[]{:S(2)}, u32[]{:S(2)}) collective-permute-start(bf16[4,64,64]{2,1,0:T(8,128)(2,1)S(1)} %get-tuple-element.13), channel_id=1, source_target_pairs={{8,0},{16,8},{24,16},{32,24},{40,32},{48,40},{56,48},{64,56},{72,6... | collective-permute-start | bytes 98312 | tf_op jit(solution)/shard_map/ppermute | solution.py:147
  39.2 1.4 %reshape.70 = f32[64,27,64]{2,1,0:T(8,128)S(1)} reshape(f32[64,1728]{1,0:T(8,128)} %get-tuple-element.10) | data formatting | bytes 884736 | tf_op jit(solution)/shard_map/reshape | solution.py:280
  40.6 0.5 copy.19
  41.1 0.0 copy-start.2
  41.1 0.2 reshape.71
  41.3 0.6 copy-done.2
  41.9 0.1 reduce
  42.0 0.8 fusion.12.x_ref
  42.8 62.3 %shard_map.104 = f32[1024,128]{1,0:T(8,128)} custom-call(f32[1024,128]{1,0:T(8,128)} %fusion.12.x_ref), custom_call_target="tpu_custom_call" | custom-call | tf_op jit(solution)/shard_map/pallas_call | solution.py:246
  105.1 0.0 copy-start.1
  105.1 1.1 slice_multiply_fusion
  106.2 1.2 slice_multiply_fusion.1
  107.4 1.1 mul.32
  108.5 0.0 collective-permute-done.2
  108.5 0.0 collective-permute-done.3
  108.6 0.0 copy-done.1
  108.6 1.1 fusion.11.g_ref
  109.6 13.9 %shard_map.103 = bf16[4,64,512]{2,1,0:T(8,128)(2,1)} custom-call(s32[104]{0:T(128)} %compare_select_fusion.tbl_ref, bf16[13,64,512]{2,1,0:T(8,128)(2,1)} %fusion.11.g_ref, bf16[4,64,512]{2,1,0:T(8,128)(2,1)} %bitcast.25, f32[4,1,512]{2,1,0:T(1,128)} %bitcast.28, bf16[64,1728]{1,0:T(8,128)(2,1)} %copy.20.wt_ref), custom_call_target="tpu_custom_call" | custom-call | tf_op jit(solution)/shard_map/pallas_call | solution.py:129
  (1 shorter events, 0.0 us)
Async XLA Ops:
  0.6 12.3 %copy-start = (bf16[27,64,64]{2,1,0:T(8,128)(2,1)S(1)}, bf16[27,64,64]{2,1,0:T(8,128)(2,1)}, u32[]{:S(2)}) copy-start(bf16[27,64,64]{2,1,0:T(8,128)(2,1)} %param.9) | copy-start | bytes 663556
  2.5 12.8 %collective-permute-start = (bf16[4,64,64]{2,1,0:T(8,128)(2,1)S(1)}, bf16[4,64,64]{2,1,0:T(8,128)(2,1)S(1)}, u32[]{:S(2)}, u32[]{:S(2)}) collective-permute-start(bf16[4,64,64]{2,1,0:T(8,128)(2,1)S(1)} %get-tuple-element.14), channel_id=1, source_target_pairs={{0,8},{8,16},{16,24},{24,32},{32,40},{40,48},{48,56},{56,64},{64,7... | collective-permute-start | bytes 98312 | tf_op jit(solution)/shard_map/ppermute | solution.py:146
  6.9 8.4 %collective-permute-start.1 = (bf16[4,64,64]{2,1,0:T(8,128)(2,1)S(1)}, bf16[4,64,64]{2,1,0:T(8,128)(2,1)S(1)}, u32[]{:S(2)}, u32[]{:S(2)}) collective-permute-start(bf16[4,64,64]{2,1,0:T(8,128)(2,1)S(1)} %get-tuple-element.15), channel_id=1, source_target_pairs={{8,0},{16,8},{24,16},{32,24},{40,32},{48,40},{56,48},{64,56},{72,6... | collective-permute-start | bytes 98312 | tf_op jit(solution)/shard_map/ppermute | solution.py:147
  33.7 74.9 %collective-permute-start.2 = (bf16[4,64,64]{2,1,0:T(8,128)(2,1)S(1)}, bf16[4,64,64]{2,1,0:T(8,128)(2,1)S(1)}, u32[]{:S(2)}, u32[]{:S(2)}) collective-permute-start(bf16[4,64,64]{2,1,0:T(8,128)(2,1)S(1)} %get-tuple-element.12), channel_id=1, source_target_pairs={{0,8},{8,16},{16,24},{24,32},{32,40},{40,48},{48,56},{56,64},{64,7... | collective-permute-start | bytes 98312 | tf_op jit(solution)/shard_map/ppermute | solution.py:146
  37.9 70.7 %collective-permute-start.3 = (bf16[4,64,64]{2,1,0:T(8,128)(2,1)S(1)}, bf16[4,64,64]{2,1,0:T(8,128)(2,1)S(1)}, u32[]{:S(2)}, u32[]{:S(2)}) collective-permute-start(bf16[4,64,64]{2,1,0:T(8,128)(2,1)S(1)} %get-tuple-element.13), channel_id=1, source_target_pairs={{8,0},{16,8},{24,16},{32,24},{40,32},{48,40},{56,48},{64,56},{72,6... | collective-permute-start | bytes 98312 | tf_op jit(solution)/shard_map/ppermute | solution.py:147
  41.1 0.8 copy-start.2
  105.1 3.4 %copy-start.1 = (bf16[4,64,512]{2,1,0:T(8,128)(2,1)S(1)}, bf16[4,64,512]{2,1,0:T(8,128)(2,1)}, u32[]{:S(2)}) copy-start(bf16[4,64,512]{2,1,0:T(8,128)(2,1)} %get-tuple-element.9) | copy-start | bytes 786436

commit v2 on v1

--- a/solution.py
+++ b/solution.py
@@ -89,18 +89,11 @@
     lax.fori_loop(0, slots, brick_step, 0)
 
 
-def backward_kernel(tbl_ref, g_ref, cot_ref, occ_ref, wt_ref, in_grad_ref, col_ref):
-    slots, channels, voxels = cot_ref.shape
-    edges = edge_masks((channels, voxels))
-
-    def brick_step(brick, carry):
-        gather_columns(g_ref, tbl_ref, brick, col_ref, -1, edges)
-        back = jnp.dot(wt_ref[...], col_ref[...], preferred_element_type=jnp.float32)
-        keep = occ_ref[brick]
-        in_grad_ref[brick] = (keep * (cot_ref[brick].astype(jnp.float32) + back)).astype(in_grad_ref.dtype)
-        return carry
-
-    lax.fori_loop(0, slots, brick_step, 0)
+def backward_brick(tbl_ref, g_ref, cot_ref, occ_ref, wt_ref, in_grad_ref, col_ref, edges, brick):
+    gather_columns(g_ref, tbl_ref, brick, col_ref, -1, edges)
+    back = jnp.dot(wt_ref[...], col_ref[...], preferred_element_type=jnp.float32)
+    keep = occ_ref[brick]
+    in_grad_ref[brick] = (keep * (cot_ref[brick].astype(jnp.float32) + back)).astype(in_grad_ref.dtype)
 
 
 def vmem_specs(n):
@@ -124,18 +117,6 @@
     )(tbl, table, cot, occ, w_all, bias)
 
 
-def run_backward(tbl, table, cot, occ, w_t):
-    slots, channels, voxels = cot.shape
-    return pl.pallas_call(
-        backward_kernel,
-        out_shape=jax.ShapeDtypeStruct((slots, channels, voxels), jnp.bfloat16),
-        in_specs=[pl.BlockSpec(memory_space=pltpu.SMEM)] + vmem_specs(4),
-        out_specs=pl.BlockSpec(memory_space=pltpu.VMEM),
-        scratch_shapes=[pltpu.VMEM((27 * channels, voxels), jnp.bfloat16)],
-        interpret=INTERPRET,
-    )(tbl, table, cot, occ, w_t)
-
-
 def exchange_planes(field):
     size = lax.axis_size("space")
     up = [(i, i + 1) for i in range(size - 1)]
@@ -170,8 +151,13 @@
     return own, (other // rep_size, other % rep_size)
 
 
-def reduce_kernel(bits, rep_size, x_ref, o_ref, buf, recv, full, send_sem, recv_sem, local_sem):
+def reduce_kernel(
+    bits, rep_size, tbl_ref, x_ref, g_ref, cot_ref, occ_ref, wt_ref, o_ref, in_grad_ref,
+    buf, recv, full, col_ref, send_sem, recv_sem, local_sem,
+):
     rows = buf.shape[0]
+    slots, channels, voxels = cot_ref.shape
+    edges = edge_masks((channels, voxels))
     me = lax.axis_index("space") * rep_size + lax.axis_index("rep")
     mesh_ids = pl.DeviceIdType.MESH
     barrier = pltpu.get_barrier_semaphore()
@@ -198,6 +184,8 @@
             device_id_type=mesh_ids,
         )
         copy.start()
+        for brick in range(step, slots, len(bits) - 1) if step < slots else ():
+            backward_brick(tbl_ref, g_ref, cot_ref, occ_ref, wt_ref, in_grad_ref, col_ref, edges, brick)
         copy.wait()
         buf[pl.ds(keep_lo, half)] += recv[pl.ds(at, half)]
         lo = keep_lo
@@ -233,7 +221,7 @@
     o_ref[...] = full[...]
 
 
-def all_sum(weight_terms, bias_terms):
+def all_sum_and_backward(weight_terms, bias_terms, tbl, grad_table, incoming, keep_float, w_t):
     flat = jnp.concatenate([weight_terms.reshape(-1), bias_terms])
     count = lax.axis_size(SUM_AXES)
     rep_size = lax.axis_size("rep")
@@ -243,24 +231,29 @@
     rows = -(-(-(-whole // 128)) // unit) * unit
     x = jnp.pad(flat, (0, rows * 128 - whole)).reshape(rows, 128)
     steps = 2 * len(bits) - 1
-    summed = pl.pallas_call(
+    slots, channels, voxels = incoming.shape
+    summed, in_grad = pl.pallas_call(
         functools.partial(reduce_kernel, bits, rep_size),
-        out_shape=jax.ShapeDtypeStruct((rows, 128), jnp.float32),
-        in_specs=[pl.BlockSpec(memory_space=pltpu.VMEM)],
-        out_specs=pl.BlockSpec(memory_space=pltpu.VMEM),
+        out_shape=(
+            jax.ShapeDtypeStruct((rows, 128), jnp.float32),
+            jax.ShapeDtypeStruct((slots, channels, voxels), jnp.bfloat16),
+        ),
+        in_specs=[pl.BlockSpec(memory_space=pltpu.SMEM)] + vmem_specs(5),
+        out_specs=tuple(vmem_specs(2)),
         scratch_shapes=[
             pltpu.VMEM((rows, 128), jnp.float32),
             pltpu.VMEM((rows, 128), jnp.float32),
             pltpu.VMEM((rows, 128), jnp.float32),
+            pltpu.VMEM((27 * channels, voxels), jnp.bfloat16),
             pltpu.SemaphoreType.DMA((steps,)),
             pltpu.SemaphoreType.DMA((steps,)),
             pltpu.SemaphoreType.DMA(()),
         ],
         compiler_params=pltpu.CompilerParams(collective_id=0, has_side_effects=True),
         interpret=REMOTE_INTERPRET,
-    )(x)
+    )(tbl, x, grad_table, incoming, keep_float, w_t)
     x = summed.reshape(-1)[:whole]
-    return x[: weight_terms.size].reshape(weight_terms.shape), x[weight_terms.size :]
+    return x[: weight_terms.size].reshape(weight_terms.shape), x[weight_terms.size :], in_grad
 
 
 def on_device(feats, cotangent, weight, bias, neighbours, occupancy):
@@ -276,9 +269,10 @@
     result, grad_pre, dw, db = run_forward(
         tbl, exchange_planes(masked), incoming, keep_float, w_all, bias.reshape(channels, 1)
     )
-    in_grad = run_backward(tbl, exchange_planes(grad_pre), incoming, keep_float, w_t)
     weight_terms = dw.reshape(channels, 27, channels).transpose(1, 0, 2)
-    weight_total, bias_total = all_sum(weight_terms, db.reshape(channels))
+    weight_total, bias_total, in_grad = all_sum_and_backward(
+        weight_terms, db.reshape(channels), tbl, exchange_planes(grad_pre), incoming, keep_float, w_t
+    )
     normaliser = 1.0 / math.sqrt(
         feats.shape[0] * lax.axis_size("rep") * slot_count * lax.axis_size("space") * 512
     )

time: 124 us -> 116 us (0.935)
  Pallas kernels: 92.6 us -> 84.1 us
    pallas_call x2 -> x1, Pallas kernels: 76.2 us -> 67.8 us  [all_sum_and_backward(): pl.pallas_call(functools.partial(reduce_kernel, bits, rep_size), out_shap...]
  transfers between devices with their start and end apart: 4 -> 4, of which waited for: 0 -> 1; matrix products, arithmetic and copies ran while one was open for 11% -> 6% of each run, Pallas kernels for 50% -> 0%
where the time goes in v2:
time: 116 us; the launch traced here: 115 us
  Pallas kernels  84.1 us (72%)
  starting transfers between devices  11.8 us (10%)
  local copies, waits for them, and re-layouts  10.1 us (9%)
  other arithmetic  8.26 us (7%)
    pallas_call x1, Pallas kernels, all_sum_and_backward(): pl.pallas_call(functools.partial(reduce_kernel, bits, rep_size), out_shap...  67.8 us
    pallas_call x1, Pallas kernels, run_forward(): pl.pallas_call(forward_kernel, out_shape=(jax.ShapeDtypeStruct((slots, ch...  16.4 us
    ppermute x2, starting transfers between devices, exchange_planes(): from_left = lax.ppermute(high, 'space', up)  9.18 us
    ppermute x2, starting transfers between devices, exchange_planes(): from_right = lax.ppermute(low, 'space', down)  2.58 us
  transfers between devices with their start and end apart: 4, of which 1 were waited for; matrix products, arithmetic and copies ran while one was open for 6% of the time, Pallas kernels for 0%

profile of v2, /device:TPU:1, one launch (start us, length us, event | category | flops | bytes accessed | tf_op | source)
XLA Modules:
  0.0 115.4 jit_solution(11134954755593490790)
XLA Ops:
  0.6 0.0 copy-start
  0.6 0.8 fusion.15
  1.4 1.0 bitcast_multiply_fusion
  2.4 0.0 copy-start.4
  2.4 0.1 fusion.14
  2.5 1.3 %collective-permute-start.1 = (bf16[4,64,64]{2,1,0:T(8,128)(2,1)S(1)}, bf16[4,64,64]{2,1,0:T(8,128)(2,1)S(1)}, u32[]{:S(2)}, u32[]{:S(2)}) collective-permute-start(bf16[4,64,64]{2,1,0:T(8,128)(2,1)S(1)} %get-tuple-element.19), channel_id=1, source_target_pairs={{8,0},{16,8},{24,16},{32,24},{40,32},{48,40},{56,48},{64,56},{72,6... | collective-permute-start | bytes 98312 | tf_op jit(solution)/shard_map/ppermute | solution.py:128
  3.8 5.0 %collective-permute-start = (bf16[4,64,64]{2,1,0:T(8,128)(2,1)S(1)}, bf16[4,64,64]{2,1,0:T(8,128)(2,1)S(1)}, u32[]{:S(2)}, u32[]{:S(2)}) collective-permute-start(bf16[4,64,64]{2,1,0:T(8,128)(2,1)S(1)} %get-tuple-element.18), channel_id=1, source_target_pairs={{0,8},{8,16},{16,24},{24,32},{32,40},{40,48},{48,56},{56,64},{64,7... | collective-permute-start | bytes 98312 | tf_op jit(solution)/shard_map/ppermute | solution.py:127
  8.8 0.8 squeeze.10
  9.6 0.7 add.28
  10.2 0.1 add.29
  10.3 0.7 add_multiply_fusion
  11.0 0.1 sub.12
  11.1 0.5 compare_select_fusion.tbl_ref
  11.6 0.6 copy.23
  12.2 0.0 copy-done
  12.2 0.3 copy.16
  12.5 1.1 reshape.67.w_ref
  13.6 0.0 copy-done.4
  13.6 0.7 copy.17.bias_ref
  14.3 0.9 copy.20.wt_ref
  15.2 0.1 pad.32.clone
  15.2 0.0 collective-permute-done.1
  15.3 0.0 collective-permute-done
  15.3 1.1 fusion.8.x_ref
  16.3 16.4 %shard_map.102 = (bf16[4,64,512]{2,1,0:T(8,128)(2,1)}, bf16[4,64,512]{2,1,0:T(8,128)(2,1)}, f32[64,1728]{1,0:T(8,128)}, f32[64,1]{1,0:T(8,128)}) custom-call(s32[104]{0:T(128)} %compare_select_fusion.tbl_ref, bf16[13,64,512]{2,1,0:T(8,128)(2,1)} %fusion.8.x_ref, bf16[4,64,512]{2,1,0:T(8,128)(2,1)} %bitcast.23, f32[4,1,512]{2,1,0:T(1,128)} %bitcast.27, ...), custom_call_target="tpu_custom_call" | custom-call | tf_op jit(solution)/shard_map/pallas_call | solution.py:105
  32.7 1.4 %reshape.69 = f32[64,27,64]{2,1,0:T(8,128)S(1)} reshape(f32[64,1728]{1,0:T(8,128)} %get-tuple-element.11) | data formatting | bytes 884736 | tf_op jit(solution)/shard_map/reshape | solution.py:272
  34.1 0.5 copy.18
  34.7 0.0 copy-start.1
  34.7 0.0 copy-start.3
  34.7 0.2 reshape.70
  34.9 0.7 copy-done.1
  35.6 0.1 fusion.13
  35.7 1.3 %collective-permute-start.3 = (bf16[4,64,64]{2,1,0:T(8,128)(2,1)S(1)}, bf16[4,64,64]{2,1,0:T(8,128)(2,1)S(1)}, u32[]{:S(2)}, u32[]{:S(2)}) collective-permute-start(bf16[4,64,64]{2,1,0:T(8,128)(2,1)S(1)} %get-tuple-element.17), channel_id=1, source_target_pairs={{8,0},{16,8},{24,16},{32,24},{40,32},{48,40},{56,48},{64,56},{72,6... | collective-permute-start | bytes 98312 | tf_op jit(solution)/shard_map/ppermute | solution.py:128
  37.0 4.2 %collective-permute-start.2 = (bf16[4,64,64]{2,1,0:T(8,128)(2,1)S(1)}, bf16[4,64,64]{2,1,0:T(8,128)(2,1)S(1)}, u32[]{:S(2)}, u32[]{:S(2)}) collective-permute-start(bf16[4,64,64]{2,1,0:T(8,128)(2,1)S(1)} %get-tuple-element.16), channel_id=1, source_target_pairs={{0,8},{8,16},{16,24},{24,32},{32,40},{40,48},{48,56},{56,64},{64,7... | collective-permute-start | bytes 98312 | tf_op jit(solution)/shard_map/ppermute | solution.py:127
  41.2 0.0 copy-done.3
  41.2 0.1 reduce
  41.3 0.8 fusion.12.x_ref
  42.1 0.0 collective-permute-done.3
  42.1 0.4 collective-permute-done.2
  42.5 1.1 fusion.11.g_ref
  43.5 67.8 %shard_map.103 = (f32[1024,128]{1,0:T(8,128)}, bf16[4,64,512]{2,1,0:T(8,128)(2,1)}) custom-call(s32[104]{0:T(128)} %compare_select_fusion.tbl_ref, f32[1024,128]{1,0:T(8,128)} %fusion.12.x_ref, bf16[13,64,512]{2,1,0:T(8,128)(2,1)} %fusion.11.g_ref, bf16[4,64,512]{2,1,0:T(8,128)(2,1)} %bitcast.24, f32[4,1,512]{2,1,0:T(1,128)} %bitcast.28, ...), custom_call_target="tpu_custom_call" | custom-call | tf_op jit(solution)/shard_map/pallas_call | solution.py:235
  111.3 0.0 copy-start.2
  111.3 1.1 slice_multiply_fusion
  112.4 1.1 mul.32
  113.5 1.2 %slice_multiply_fusion.1 = f32[64]{0:T(128)} fusion(f32[131072]{0:T(1024)} %bitcast.25), kind=kLoop, calls=%fused_computation.24 | loop fusion | flops 64 | bytes 512 | tf_op jit(solution)/shard_map/mul | solution.py:279
  114.7 0.0 copy-done.2
  114.7 0.7 copy.25
  (1 shorter events, 0.0 us)
Async XLA Ops:
  0.6 11.6 %copy-start = (bf16[27,64,64]{2,1,0:T(8,128)(2,1)S(1)}, bf16[27,64,64]{2,1,0:T(8,128)(2,1)}, u32[]{:S(2)}) copy-start(bf16[27,64,64]{2,1,0:T(8,128)(2,1)} %param.9) | copy-start | bytes 663556
  2.4 11.2 %copy-start.4 = (f32[64]{0:T(128)S(1)}, f32[64]{0:T(128)}, u32[]{:S(2)}) copy-start(f32[64]{0:T(128)} %param.10) | copy-start | bytes 772
  2.5 12.8 %collective-permute-start.1 = (bf16[4,64,64]{2,1,0:T(8,128)(2,1)S(1)}, bf16[4,64,64]{2,1,0:T(8,128)(2,1)S(1)}, u32[]{:S(2)}, u32[]{:S(2)}) collective-permute-start(bf16[4,64,64]{2,1,0:T(8,128)(2,1)S(1)} %get-tuple-element.19), channel_id=1, source_target_pairs={{8,0},{16,8},{24,16},{32,24},{40,32},{48,40},{56,48},{64,56},{72,6... | collective-permute-start | bytes 98312 | tf_op jit(solution)/shard_map/ppermute | solution.py:128
  3.8 11.5 %collective-permute-start = (bf16[4,64,64]{2,1,0:T(8,128)(2,1)S(1)}, bf16[4,64,64]{2,1,0:T(8,128)(2,1)S(1)}, u32[]{:S(2)}, u32[]{:S(2)}) collective-permute-start(bf16[4,64,64]{2,1,0:T(8,128)(2,1)S(1)} %get-tuple-element.18), channel_id=1, source_target_pairs={{0,8},{8,16},{16,24},{24,32},{32,40},{40,48},{48,56},{56,64},{64,7... | collective-permute-start | bytes 98312 | tf_op jit(solution)/shard_map/ppermute | solution.py:127
  34.7 1.0 copy-start.1
  34.7 6.5 %copy-start.3 = (f32[64,1]{1,0:T(8,128)S(1)}, f32[64,1]{1,0:T(8,128)}, u32[]{:S(2)}) copy-start(f32[64,1]{1,0:T(8,128)} %get-tuple-element.12) | copy-start | bytes 772
  35.7 6.4 %collective-permute-start.3 = (bf16[4,64,64]{2,1,0:T(8,128)(2,1)S(1)}, bf16[4,64,64]{2,1,0:T(8,128)(2,1)S(1)}, u32[]{:S(2)}, u32[]{:S(2)}) collective-permute-start(bf16[4,64,64]{2,1,0:T(8,128)(2,1)S(1)} %get-tuple-element.17), channel_id=1, source_target_pairs={{8,0},{16,8},{24,16},{32,24},{40,32},{48,40},{56,48},{64,56},{72,6... | collective-permute-start | bytes 98312 | tf_op jit(solution)/shard_map/ppermute | solution.py:128
  37.0 5.5 %collective-permute-start.2 = (bf16[4,64,64]{2,1,0:T(8,128)(2,1)S(1)}, bf16[4,64,64]{2,1,0:T(8,128)(2,1)S(1)}, u32[]{:S(2)}, u32[]{:S(2)}) collective-permute-start(bf16[4,64,64]{2,1,0:T(8,128)(2,1)S(1)} %get-tuple-element.16), channel_id=1, source_target_pairs={{0,8},{8,16},{16,24},{24,32},{32,40},{40,48},{48,56},{56,64},{64,7... | collective-permute-start | bytes 98312 | tf_op jit(solution)/shard_map/ppermute | solution.py:127
  111.3 3.4 %copy-start.2 = (bf16[4,64,512]{2,1,0:T(8,128)(2,1)S(1)}, bf16[4,64,512]{2,1,0:T(8,128)(2,1)}, u32[]{:S(2)}) copy-start(bf16[4,64,512]{2,1,0:T(8,128)(2,1)} %get-tuple-element.14) | copy-start | bytes 786436

commit v3 on v2

--- a/solution.py
+++ b/solution.py
@@ -38,10 +38,10 @@
         val = None
         for direction, roll, pattern in offset_terms(shift):
             if direction == (0, 0, 0):
-                field = src_ref[brick].astype(jnp.float32)
+                field = src_ref[brick]
             else:
                 slot = tbl_ref[base + DIRECTIONS.index(direction)]
-                field = src_ref[slot].astype(jnp.float32)
+                field = src_ref[slot]
             if roll:
                 field = pltpu.roll(field, roll, 1)
             if val is None:
@@ -52,7 +52,7 @@
                 m = edges[(axis, step)] if out else jnp.logical_not(edges[(axis, step)])
                 mask = m if mask is None else jnp.logical_and(mask, m)
             val = jnp.where(mask, field, val)
-        col_ref[pl.ds(k * 64, 64), :] = val.astype(jnp.bfloat16)
+        col_ref[pl.ds(k * 64, 64), :] = val
 
 
 def edge_masks(shape):
@@ -67,7 +67,7 @@
 
 def forward_kernel(tbl_ref, x_ref, cot_ref, occ_ref, w_ref, bias_ref, out_ref, gp_ref, dw_ref, db_ref, col_ref):
     slots, channels, voxels = cot_ref.shape
-    edges = edge_masks((channels, voxels))
+    edges = edge_masks((1, voxels))
     dw_ref[...] = jnp.zeros_like(dw_ref)
     db_ref[...] = jnp.zeros_like(db_ref)
 
@@ -142,98 +142,139 @@
 
 
 SUM_AXES = ("space", "rep")
-SUM_ORDER = (0, 1, 3, 6, 2, 4, 7, 5)
-
-
-def partner_of(me, bit, rep_size):
-    own = (me // (1 << bit)) % 2
-    other = me + (1 - 2 * own) * (1 << bit)
-    return own, (other // rep_size, other % rep_size)
+
+
+def sum_levels(space_size, rep_size):
+    z_size = 8 if space_size % 8 == 0 else space_size
+    space_i = lax.axis_index("space")
+    rep_i = lax.axis_index("rep")
+    x_i, z_i = space_i // z_size, space_i % z_size
+    levels = []
+    if rep_size > 1:
+        levels.append((rep_size, rep_i, lambda p: (space_i, p)))
+    if z_size > 1:
+        levels.append((z_size, z_i, lambda p: (x_i * z_size + p, rep_i)))
+    if space_size // z_size > 1:
+        levels.append((space_size // z_size, x_i, lambda p: (p * z_size + z_i, rep_i)))
+    return levels
 
 
 def reduce_kernel(
-    bits, rep_size, tbl_ref, x_ref, g_ref, cot_ref, occ_ref, wt_ref, o_ref, in_grad_ref,
-    buf, recv, full, col_ref, send_sem, recv_sem, local_sem,
+    space_size, rep_size, tbl_ref, x_ref, g_ref, cot_ref, occ_ref, wt_ref, o_ref, in_grad_ref, *scratch,
 ):
+    levels = sum_levels(space_size, rep_size)
+    count = len(levels)
+    buf, full, col_ref, send_sem, recv_sem, local_sem = scratch[:6]
+    recvs = scratch[6:]
     rows = buf.shape[0]
     slots, channels, voxels = cot_ref.shape
-    edges = edge_masks((channels, voxels))
-    me = lax.axis_index("space") * rep_size + lax.axis_index("rep")
+    edges = edge_masks((1, voxels))
+    windows = 2 * count - 1
     mesh_ids = pl.DeviceIdType.MESH
+
+    def bricks_of(window):
+        for brick in range(window, slots, windows):
+            backward_brick(tbl_ref, g_ref, cot_ref, occ_ref, wt_ref, in_grad_ref, col_ref, edges, brick)
+
     barrier = pltpu.get_barrier_semaphore()
-    for bit in bits:
-        pl.semaphore_signal(barrier, 1, device_id=partner_of(me, bit, rep_size)[1], device_id_type=mesh_ids)
-    pl.semaphore_wait(barrier, len(bits))
+    for n, r, device in levels:
+        for d in range(1, n):
+            pl.semaphore_signal(barrier, 1, device_id=device((r + d) % n), device_id_type=mesh_ids)
+    pl.semaphore_wait(barrier, sum(n - 1 for n, _, _ in levels))
     first = pltpu.make_async_copy(x_ref, buf, local_sem)
     first.start()
     first.wait()
     lo = 0
     length = rows
-    for step, bit in enumerate(bits[:-1]):
-        own, device = partner_of(me, bit, rep_size)
-        half = length // 2
-        keep_lo = pl.multiple_of(lo + own * half, 8)
-        send_lo = pl.multiple_of(lo + (1 - own) * half, 8)
-        at = rows - (rows >> step)
+    for i, (n, r, device) in enumerate(levels[:-1]):
+        chunk = length // n
+        copies = []
+        for d in range(1, n):
+            p = (r + d) % n
+            copy = pltpu.make_async_remote_copy(
+                src_ref=buf.at[pl.ds(pl.multiple_of(lo + p * chunk, 8), chunk)],
+                dst_ref=recvs[i].at[d],
+                send_sem=send_sem.at[i, d],
+                recv_sem=recv_sem.at[i, d],
+                device_id=device(p),
+                device_id_type=mesh_ids,
+            )
+            copy.start()
+            copies.append(copy)
+        bricks_of(i)
+        for copy in copies:
+            copy.wait()
+        mine = pl.multiple_of(lo + r * chunk, 8)
+        total = buf[pl.ds(mine, chunk)]
+        for d in range(1, n):
+            total = total + recvs[i][d]
+        buf[pl.ds(mine, chunk)] = total
+        lo = mine
+        length = chunk
+    last = count - 1
+    n, r, device = levels[last]
+    stage = recvs[last]
+    stage[0] = buf[pl.ds(lo, length)]
+    copies = []
+    for d in range(1, n):
         copy = pltpu.make_async_remote_copy(
-            src_ref=buf.at[pl.ds(send_lo, half)],
-            dst_ref=recv.at[pl.ds(at, half)],
-            send_sem=send_sem.at[step],
-            recv_sem=recv_sem.at[step],
-            device_id=device,
+            src_ref=buf.at[pl.ds(lo, length)],
+            dst_ref=stage.at[d],
+            send_sem=send_sem.at[last, d],
+            recv_sem=recv_sem.at[last, d],
+            device_id=device((r + d) % n),
             device_id_type=mesh_ids,
         )
         copy.start()
-        for brick in range(step, slots, len(bits) - 1) if step < slots else ():
-            backward_brick(tbl_ref, g_ref, cot_ref, occ_ref, wt_ref, in_grad_ref, col_ref, edges, brick)
+        copies.append(copy)
+    bricks_of(last)
+    for copy in copies:
         copy.wait()
-        buf[pl.ds(keep_lo, half)] += recv[pl.ds(at, half)]
-        lo = keep_lo
-        length = half
-    last = len(bits) - 1
-    own, device = partner_of(me, bits[last], rep_size)
-    at = rows - length
-    copy = pltpu.make_async_remote_copy(
-        src_ref=buf.at[pl.ds(lo, length)],
-        dst_ref=recv.at[pl.ds(at, length)],
-        send_sem=send_sem.at[last],
-        recv_sem=recv_sem.at[last],
-        device_id=device,
-        device_id_type=mesh_ids,
-    )
-    copy.start()
-    copy.wait()
-    full[pl.ds(lo, length)] = buf[pl.ds(lo, length)] + recv[pl.ds(at, length)]
-    for step in reversed(range(last)):
-        own, device = partner_of(me, bits[step], rep_size)
-        copy = pltpu.make_async_remote_copy(
-            src_ref=full.at[pl.ds(lo, length)],
-            dst_ref=full.at[pl.ds(lo, length)],
-            send_sem=send_sem.at[last + 1 + step],
-            recv_sem=recv_sem.at[last + 1 + step],
-            device_id=device,
-            device_id_type=mesh_ids,
-        )
-        copy.start()
-        copy.wait()
-        lo = pl.multiple_of(lo - own * length, 8)
-        length = 2 * length
+    total = stage[(r + n) % n]
+    for m in range(1, n):
+        total = total + stage[(r + n - m) % n]
+    full[pl.ds(lo, length)] = total
+    for i in reversed(range(last)):
+        n, r, device = levels[i]
+        copies = []
+        for d in range(1, n):
+            copy = pltpu.make_async_remote_copy(
+                src_ref=full.at[pl.ds(lo, length)],
+                dst_ref=full.at[pl.ds(lo, length)],
+                send_sem=send_sem.at[count + i, d],
+                recv_sem=recv_sem.at[count + i, d],
+                device_id=device((r + d) % n),
+                device_id_type=mesh_ids,
+            )
+            copy.start()
+            copies.append(copy)
+        bricks_of(2 * count - 1 - 1 - i)
+        for copy in copies:
+            copy.wait()
+        lo = pl.multiple_of(lo - r * length, 8)
+        length = n * length
     o_ref[...] = full[...]
 
 
 def all_sum_and_backward(weight_terms, bias_terms, tbl, grad_table, incoming, keep_float, w_t):
     flat = jnp.concatenate([weight_terms.reshape(-1), bias_terms])
-    count = lax.axis_size(SUM_AXES)
+    space_size = lax.axis_size("space")
     rep_size = lax.axis_size("rep")
-    bits = tuple(b for b in SUM_ORDER if (1 << b) < count)
-    unit = 8 << (len(bits) - 1)
+    z_size = 8 if space_size % 8 == 0 else space_size
+    sizes = [n for n in (rep_size, z_size, space_size // z_size) if n > 1]
+    unit = 8 * math.prod(sizes[:-1])
     whole = flat.shape[0]
     rows = -(-(-(-whole // 128)) // unit) * unit
     x = jnp.pad(flat, (0, rows * 128 - whole)).reshape(rows, 128)
-    steps = 2 * len(bits) - 1
+    recvs = []
+    length = rows
+    for n in sizes[:-1]:
+        length //= n
+        recvs.append(pltpu.VMEM((n, length, 128), jnp.float32))
+    recvs.append(pltpu.VMEM((sizes[-1], length, 128), jnp.float32))
     slots, channels, voxels = incoming.shape
     summed, in_grad = pl.pallas_call(
-        functools.partial(reduce_kernel, bits, rep_size),
+        functools.partial(reduce_kernel, space_size, rep_size),
         out_shape=(
             jax.ShapeDtypeStruct((rows, 128), jnp.float32),
             jax.ShapeDtypeStruct((slots, channels, voxels), jnp.bfloat16),
@@ -243,12 +284,12 @@
         scratch_shapes=[
             pltpu.VMEM((rows, 128), jnp.float32),
             pltpu.VMEM((rows, 128), jnp.float32),
-            pltpu.VMEM((rows, 128), jnp.float32),
             pltpu.VMEM((27 * channels, voxels), jnp.bfloat16),
-            pltpu.SemaphoreType.DMA((steps,)),
-            pltpu.SemaphoreType.DMA((steps,)),
+            pltpu.SemaphoreType.DMA((2 * len(sizes), max(sizes))),
+            pltpu.SemaphoreType.DMA((2 * len(sizes), max(sizes))),
             pltpu.SemaphoreType.DMA(()),
-        ],
+        ]
+        + recvs,
         compiler_params=pltpu.CompilerParams(collective_id=0, has_side_effects=True),
         interpret=REMOTE_INTERPRET,
     )(tbl, x, grad_table, incoming, keep_float, w_t)

time: 116 us -> 93.4 us (0.81)
  Pallas kernels: 84.1 us -> 61.7 us
    pallas_call x1, Pallas kernels: 67.8 us -> 47.7 us  [all_sum_and_backward(): pl.pallas_call(functools.partial(reduce_kernel, space_size, rep_size), ou...]
    pallas_call x1, Pallas kernels: 16.4 us -> 14 us  [run_forward(): pl.pallas_call(forward_kernel, out_shape=(jax.ShapeDtypeStruct((slots, ch...]
  transfers between devices with their start and end apart: 4 -> 4, of which waited for: 1 -> 1; matrix products, arithmetic and copies ran while one was open for 6% -> 8% of each run, Pallas kernels for 0% -> 0%
where the time goes in v3:
time: 93.4 us; the launch traced here: 93 us
  Pallas kernels  61.7 us (66%)
  starting transfers between devices  11.9 us (13%)
  local copies, waits for them, and re-layouts  10.1 us (11%)
  other arithmetic  8.26 us (9%)
    pallas_call x1, Pallas kernels, all_sum_and_backward(): pl.pallas_call(functools.partial(reduce_kernel, space_size, rep_size), ou...  47.7 us
    pallas_call x1, Pallas kernels, run_forward(): pl.pallas_call(forward_kernel, out_shape=(jax.ShapeDtypeStruct((slots, ch...  14 us
    ppermute x2, starting transfers between devices, exchange_planes(): from_left = lax.ppermute(high, 'space', up)  9.35 us
    ppermute x2, starting transfers between devices, exchange_planes(): from_right = lax.ppermute(low, 'space', down)  2.58 us
    concatenate x2, other arithmetic, exchange_planes(): return jnp.concatenate([field, left, right, zero])  2.1 us
    unnamed x12, local copies, waits for them, and re-layouts  2.07 us
  transfers between devices with their start and end apart: 4, of which 1 were waited for; matrix products, arithmetic and copies ran while one was open for 8% of the time, Pallas kernels for 0%

profile of v3, /device:TPU:1, one launch (start us, length us, event | category | flops | bytes accessed | tf_op | source)
XLA Modules:
  0.0 93.0 jit_solution(5126155803751896742)
XLA Ops:
  0.6 0.0 copy-start
  0.6 0.8 fusion.15
  1.4 1.0 %bitcast_multiply_fusion = bf16[4,64,512]{2,1,0:T(8,128)(2,1)S(1)} fusion(bf16[1,4,64,512]{3,2,1,0:T(8,128)(2,1)} %param.7, bf16[4,512]{1,0:T(4,128)(2,1)S(1)} %get-tuple-element.21), kind=kLoop, calls=%fused_computation.20 | loop fusion | flops 131072 | bytes 528384 | tf_op jit(solution)/shard_map/mul | solution.py:305
  2.4 0.0 copy-start.4
  2.4 0.1 fusion.14
  2.5 1.3 %collective-permute-start.1 = (bf16[4,64,64]{2,1,0:T(8,128)(2,1)S(1)}, bf16[4,64,64]{2,1,0:T(8,128)(2,1)S(1)}, u32[]{:S(2)}, u32[]{:S(2)}) collective-permute-start(bf16[4,64,64]{2,1,0:T(8,128)(2,1)S(1)} %get-tuple-element.19), channel_id=1, source_target_pairs={{8,0},{16,8},{24,16},{32,24},{40,32},{48,40},{56,48},{64,56},{72,6... | collective-permute-start | bytes 98312 | tf_op jit(solution)/shard_map/ppermute | solution.py:128
  3.8 5.0 %collective-permute-start = (bf16[4,64,64]{2,1,0:T(8,128)(2,1)S(1)}, bf16[4,64,64]{2,1,0:T(8,128)(2,1)S(1)}, u32[]{:S(2)}, u32[]{:S(2)}) collective-permute-start(bf16[4,64,64]{2,1,0:T(8,128)(2,1)S(1)} %get-tuple-element.18), channel_id=1, source_target_pairs={{0,8},{8,16},{16,24},{24,32},{32,40},{40,48},{48,56},{56,64},{64,7... | collective-permute-start | bytes 98312 | tf_op jit(solution)/shard_map/ppermute | solution.py:127
  8.8 0.8 squeeze.10
  9.6 0.7 add.28
  10.2 0.1 add.29
  10.3 0.7 add_multiply_fusion
  11.0 0.1 sub.12
  11.1 0.5 compare_select_fusion.tbl_ref
  11.6 0.6 copy.23
  12.2 0.0 copy-done
  12.2 0.3 copy.16
  12.5 1.1 %reshape.67.w_ref = bf16[64,1728]{1,0:T(8,128)(2,1)} reshape(bf16[64,27,64]{2,1,0:T(8,128)(2,1)S(1)} %copy.16) | data formatting | bytes 442368 | tf_op jit(solution)/shard_map/reshape | solution.py:308
  13.6 0.0 copy-done.4
  13.6 0.7 copy.17.bias_ref
  14.3 0.9 copy.20.wt_ref
  15.2 0.1 pad.32.clone
  15.2 0.0 collective-permute-done.1
  15.3 0.0 collective-permute-done
  15.3 1.1 %fusion.8.x_ref = bf16[13,64,512]{2,1,0:T(8,128)(2,1)} fusion(bf16[4,64,64]{2,1,0:T(8,128)(2,1)S(1)} %collective-permute-done.1, bf16[4,64,64]{2,1,0:T(8,128)(2,1)S(1)} %collective-permute-done, bf16[4,64,512]{2,1,0:T(8,128)(2,1)S(1)} %bitcast_multiply_fusion, bf16[13]{0:T(256)(128)(2,1)S(1)} %pad.32.clone), kind=kLoop, calls=%fused_computation.12 | loop fusion | flops 6815744 | bytes 1179674 | tf_op jit(solution)/shard_map/concatenate | solution.py:132
  16.3 14.0 %shard_map.102 = (bf16[4,64,512]{2,1,0:T(8,128)(2,1)}, bf16[4,64,512]{2,1,0:T(8,128)(2,1)}, f32[64,1728]{1,0:T(8,128)}, f32[64,1]{1,0:T(8,128)}) custom-call(s32[104]{0:T(128)} %compare_select_fusion.tbl_ref, bf16[13,64,512]{2,1,0:T(8,128)(2,1)} %fusion.8.x_ref, bf16[4,64,512]{2,1,0:T(8,128)(2,1)} %bitcast.23, f32[4,1,512]{2,1,0:T(1,128)} %bitcast.27, ...), custom_call_target="tpu_custom_call" | custom-call | tf_op jit(solution)/shard_map/pallas_call | solution.py:105
  30.3 1.4 %reshape.69 = f32[64,27,64]{2,1,0:T(8,128)S(1)} reshape(f32[64,1728]{1,0:T(8,128)} %get-tuple-element.11) | data formatting | bytes 884736 | tf_op jit(solution)/shard_map/reshape | solution.py:313
  31.7 0.5 copy.18
  32.3 0.0 copy-start.1
  32.3 0.0 copy-start.3
  32.3 0.2 reshape.70
  32.5 0.7 copy-done.1
  33.2 0.1 fusion.13
  33.3 1.3 %collective-permute-start.3 = (bf16[4,64,64]{2,1,0:T(8,128)(2,1)S(1)}, bf16[4,64,64]{2,1,0:T(8,128)(2,1)S(1)}, u32[]{:S(2)}, u32[]{:S(2)}) collective-permute-start(bf16[4,64,64]{2,1,0:T(8,128)(2,1)S(1)} %get-tuple-element.17), channel_id=1, source_target_pairs={{8,0},{16,8},{24,16},{32,24},{40,32},{48,40},{56,48},{64,56},{72,6... | collective-permute-start | bytes 98312 | tf_op jit(solution)/shard_map/ppermute | solution.py:128
  34.6 4.4 %collective-permute-start.2 = (bf16[4,64,64]{2,1,0:T(8,128)(2,1)S(1)}, bf16[4,64,64]{2,1,0:T(8,128)(2,1)S(1)}, u32[]{:S(2)}, u32[]{:S(2)}) collective-permute-start(bf16[4,64,64]{2,1,0:T(8,128)(2,1)S(1)} %get-tuple-element.16), channel_id=1, source_target_pairs={{0,8},{8,16},{16,24},{24,32},{32,40},{40,48},{48,56},{56,64},{64,7... | collective-permute-start | bytes 98312 | tf_op jit(solution)/shard_map/ppermute | solution.py:127
  39.0 0.0 copy-done.3
  39.0 0.1 reduce
  39.1 0.8 fusion.12.x_ref
  39.9 0.0 collective-permute-done.3
  39.9 0.2 collective-permute-done.2
  40.1 1.1 %fusion.11.g_ref = bf16[13,64,512]{2,1,0:T(8,128)(2,1)} fusion(bf16[4,64,64]{2,1,0:T(8,128)(2,1)S(1)} %collective-permute-done.3, bf16[4,64,64]{2,1,0:T(8,128)(2,1)S(1)} %collective-permute-done.2, bf16[4,64,512]{2,1,0:T(8,128)(2,1)S(1)} %copy-done.1, bf16[13]{0:T(256)(128)(2,1)S(1)} %pad.32.clone), kind=kLoop, calls=%fused_computation.15 | loop fusion | flops 6815744 | bytes 1179674 | tf_op jit(solution)/shard_map/concatenate | solution.py:132
  41.2 47.7 %shard_map.103 = (f32[1024,128]{1,0:T(8,128)}, bf16[4,64,512]{2,1,0:T(8,128)(2,1)}) custom-call(s32[104]{0:T(128)} %compare_select_fusion.tbl_ref, f32[1024,128]{1,0:T(8,128)} %fusion.12.x_ref, bf16[13,64,512]{2,1,0:T(8,128)(2,1)} %fusion.11.g_ref, bf16[4,64,512]{2,1,0:T(8,128)(2,1)} %bitcast.24, f32[4,1,512]{2,1,0:T(1,128)} %bitcast.28, ...), custom_call_target="tpu_custom_call" | custom-call | tf_op jit(solution)/shard_map/pallas_call | solution.py:276
  88.9 0.0 copy-start.2
  88.9 1.1 %slice_multiply_fusion = f32[864,128]{1,0:T(8,128)S(1)} fusion(f32[1024,128]{1,0:T(8,128)} %get-tuple-element.15), kind=kLoop, calls=%fused_computation.19 | loop fusion | flops 110592 | bytes 884736 | tf_op jit(solution)/shard_map/mul | solution.py:320
  90.0 1.1 %mul.32 = f32[27,64,64]{2,1,0:T(8,128)} reshape(f32[864,128]{1,0:T(8,128)S(1)} %slice_multiply_fusion) | data formatting | bytes 884736 | tf_op jit(solution)/shard_map/mul | solution.py:320
  91.1 1.2 %slice_multiply_fusion.1 = f32[64]{0:T(128)} fusion(f32[131072]{0:T(1024)} %bitcast.25), kind=kLoop, calls=%fused_computation.24 | loop fusion | flops 64 | bytes 512 | tf_op jit(solution)/shard_map/mul | solution.py:320
  92.3 0.0 copy-done.2
  92.3 0.7 copy.25
  (1 shorter events, 0.0 us)
Async XLA Ops:
  0.6 11.6 %copy-start = (bf16[27,64,64]{2,1,0:T(8,128)(2,1)S(1)}, bf16[27,64,64]{2,1,0:T(8,128)(2,1)}, u32[]{:S(2)}) copy-start(bf16[27,64,64]{2,1,0:T(8,128)(2,1)} %param.9) | copy-start | bytes 663556
  2.4 11.2 %copy-start.4 = (f32[64]{0:T(128)S(1)}, f32[64]{0:T(128)}, u32[]{:S(2)}) copy-start(f32[64]{0:T(128)} %param.10) | copy-start | bytes 772
  2.5 12.8 %collective-permute-start.1 = (bf16[4,64,64]{2,1,0:T(8,128)(2,1)S(1)}, bf16[4,64,64]{2,1,0:T(8,128)(2,1)S(1)}, u32[]{:S(2)}, u32[]{:S(2)}) collective-permute-start(bf16[4,64,64]{2,1,0:T(8,128)(2,1)S(1)} %get-tuple-element.19), channel_id=1, source_target_pairs={{8,0},{16,8},{24,16},{32,24},{40,32},{48,40},{56,48},{64,56},{72,6... | collective-permute-start | bytes 98312 | tf_op jit(solution)/shard_map/ppermute | solution.py:128
  3.8 11.5 %collective-permute-start = (bf16[4,64,64]{2,1,0:T(8,128)(2,1)S(1)}, bf16[4,64,64]{2,1,0:T(8,128)(2,1)S(1)}, u32[]{:S(2)}, u32[]{:S(2)}) collective-permute-start(bf16[4,64,64]{2,1,0:T(8,128)(2,1)S(1)} %get-tuple-element.18), channel_id=1, source_target_pairs={{0,8},{8,16},{16,24},{24,32},{32,40},{40,48},{48,56},{56,64},{64,7... | collective-permute-start | bytes 98312 | tf_op jit(solution)/shard_map/ppermute | solution.py:127
  32.3 1.0 %copy-start.1 = (bf16[4,64,512]{2,1,0:T(8,128)(2,1)S(1)}, bf16[4,64,512]{2,1,0:T(8,128)(2,1)}, u32[]{:S(2)}) copy-start(bf16[4,64,512]{2,1,0:T(8,128)(2,1)} %get-tuple-element.13) | copy-start | bytes 786436
  32.3 6.7 %copy-start.3 = (f32[64,1]{1,0:T(8,128)S(1)}, f32[64,1]{1,0:T(8,128)}, u32[]{:S(2)}) copy-start(f32[64,1]{1,0:T(8,128)} %get-tuple-element.12) | copy-start | bytes 772
  33.3 6.6 %collective-permute-start.3 = (bf16[4,64,64]{2,1,0:T(8,128)(2,1)S(1)}, bf16[4,64,64]{2,1,0:T(8,128)(2,1)S(1)}, u32[]{:S(2)}, u32[]{:S(2)}) collective-permute-start(bf16[4,64,64]{2,1,0:T(8,128)(2,1)S(1)} %get-tuple-element.17), channel_id=1, source_target_pairs={{8,0},{16,8},{24,16},{32,24},{40,32},{48,40},{56,48},{64,56},{72,6... | collective-permute-start | bytes 98312 | tf_op jit(solution)/shard_map/ppermute | solution.py:128
  34.6 5.5 %collective-permute-start.2 = (bf16[4,64,64]{2,1,0:T(8,128)(2,1)S(1)}, bf16[4,64,64]{2,1,0:T(8,128)(2,1)S(1)}, u32[]{:S(2)}, u32[]{:S(2)}) collective-permute-start(bf16[4,64,64]{2,1,0:T(8,128)(2,1)S(1)} %get-tuple-element.16), channel_id=1, source_target_pairs={{0,8},{8,16},{16,24},{24,32},{32,40},{40,48},{48,56},{56,64},{64,7... | collective-permute-start | bytes 98312 | tf_op jit(solution)/shard_map/ppermute | solution.py:127
  88.9 3.4 %copy-start.2 = (bf16[4,64,512]{2,1,0:T(8,128)(2,1)S(1)}, bf16[4,64,512]{2,1,0:T(8,128)(2,1)}, u32[]{:S(2)}) copy-start(bf16[4,64,512]{2,1,0:T(8,128)(2,1)} %get-tuple-element.14) | copy-start | bytes 786436

commit v4 on v3

--- a/solution.py
+++ b/solution.py
@@ -160,12 +160,12 @@
 
 
 def reduce_kernel(
-    space_size, rep_size, tbl_ref, x_ref, g_ref, cot_ref, occ_ref, wt_ref, o_ref, in_grad_ref, *scratch,
+    space_size, rep_size, tbl_ref, x_ref, gp_ref, cot_ref, occ_ref, wt_ref, o_ref, in_grad_ref, *scratch,
 ):
     levels = sum_levels(space_size, rep_size)
     count = len(levels)
-    buf, full, col_ref, send_sem, recv_sem, local_sem = scratch[:6]
-    recvs = scratch[6:]
+    buf, full, col_ref, send_sem, recv_sem, local_sem, g_ref, plane_send, plane_recv = scratch[:9]
+    recvs = scratch[9:]
     rows = buf.shape[0]
     slots, channels, voxels = cot_ref.shape
     edges = edge_masks((1, voxels))
@@ -176,11 +176,32 @@
         for brick in range(window, slots, windows):
             backward_brick(tbl_ref, g_ref, cot_ref, occ_ref, wt_ref, in_grad_ref, col_ref, edges, brick)
 
+    space_i = lax.axis_index("space")
+    rep_i = lax.axis_index("rep")
+    sides = ((space_i + 1) % space_size, (space_i + space_size - 1) % space_size)
+    g_ref[pl.ds(slots, 2 * slots + 1)] = jnp.zeros((2 * slots + 1, channels, voxels), g_ref.dtype)
+    g_ref[pl.ds(0, slots)] = gp_ref[...]
     barrier = pltpu.get_barrier_semaphore()
     for n, r, device in levels:
         for d in range(1, n):
             pl.semaphore_signal(barrier, 1, device_id=device((r + d) % n), device_id_type=mesh_ids)
-    pl.semaphore_wait(barrier, sum(n - 1 for n, _, _ in levels))
+    for side in sides:
+        pl.semaphore_signal(barrier, 1, device_id=(side, rep_i), device_id_type=mesh_ids)
+    pl.semaphore_wait(barrier, sum(n - 1 for n, _, _ in levels) + 2)
+    planes = []
+    for way, side in enumerate(sides):
+        lanes = pl.ds(voxels - 128, 128) if way == 0 else pl.ds(0, 128)
+        for brick in range(slots):
+            copy = pltpu.make_async_remote_copy(
+                src_ref=gp_ref.at[brick, :, lanes],
+                dst_ref=g_ref.at[(way + 1) * slots + brick, :, lanes],
+                send_sem=plane_send.at[way, brick],
+                recv_sem=plane_recv.at[way, brick],
+                device_id=(side, rep_i),
+                device_id_type=mesh_ids,
+            )
+            copy.start()
+            planes.append(copy)
     first = pltpu.make_async_copy(x_ref, buf, local_sem)
     first.start()
     first.wait()
@@ -201,6 +222,9 @@
             )
             copy.start()
             copies.append(copy)
+        if i == 0:
+            for copy in planes:
+                copy.wait()
         bricks_of(i)
         for copy in copies:
             copy.wait()
@@ -256,7 +280,7 @@
     o_ref[...] = full[...]
 
 
-def all_sum_and_backward(weight_terms, bias_terms, tbl, grad_table, incoming, keep_float, w_t):
+def all_sum_and_backward(weight_terms, bias_terms, tbl, grad_pre, incoming, keep_float, w_t):
     flat = jnp.concatenate([weight_terms.reshape(-1), bias_terms])
     space_size = lax.axis_size("space")
     rep_size = lax.axis_size("rep")
@@ -288,11 +312,14 @@
             pltpu.SemaphoreType.DMA((2 * len(sizes), max(sizes))),
             pltpu.SemaphoreType.DMA((2 * len(sizes), max(sizes))),
             pltpu.SemaphoreType.DMA(()),
+            pltpu.VMEM((3 * slots + 1, channels, voxels), jnp.bfloat16),
+            pltpu.SemaphoreType.DMA((2, slots)),
+            pltpu.SemaphoreType.DMA((2, slots)),
         ]
         + recvs,
         compiler_params=pltpu.CompilerParams(collective_id=0, has_side_effects=True),
         interpret=REMOTE_INTERPRET,
-    )(tbl, x, grad_table, incoming, keep_float, w_t)
+    )(tbl, x, grad_pre, incoming, keep_float, w_t)
     x = summed.reshape(-1)[:whole]
     return x[: weight_terms.size].reshape(weight_terms.shape), x[weight_terms.size :], in_grad
 
@@ -312,7 +339,7 @@
     )
     weight_terms = dw.reshape(channels, 27, channels).transpose(1, 0, 2)
     weight_total, bias_total, in_grad = all_sum_and_backward(
-        weight_terms, db.reshape(channels), tbl, exchange_planes(grad_pre), incoming, keep_float, w_t
+        weight_terms, db.reshape(channels), tbl, grad_pre, incoming, keep_float, w_t
     )
     normaliser = 1.0 / math.sqrt(
         feats.shape[0] * lax.axis_size("rep") * slot_count * lax.axis_size("space") * 512

time: 93.4 us -> 79.7 us (0.85)
  Pallas kernels: 61.7 us -> 55.1 us
  starting transfers between devices: 11.9 us -> 6.29 us
  other arithmetic: 8.26 us -> 7.21 us
    pallas_call x1, Pallas kernels: 47.7 us -> 41.1 us  [all_sum_and_backward(): pl.pallas_call(functools.partial(reduce_kernel, space_size, rep_size), ou...]
    ppermute x2 -> x1, starting transfers between devices: 9.35 us -> 5 us  [exchange_planes(): from_left = lax.ppermute(high, 'space', up)]
    ppermute x2 -> x1, starting transfers between devices: 2.58 us -> 1.29 us  [exchange_planes(): from_right = lax.ppermute(low, 'space', down)]
    concatenate x2 -> x1, other arithmetic: 2.1 us -> 1.05 us  [exchange_planes(): return jnp.concatenate([field, left, right, zero])]
    unnamed x12 -> x10, local copies, waits for them, and re-layouts: 2.07 us -> 1.88 us
  transfers between devices with their start and end apart: 4 -> 2, of which waited for: 1 -> 0; matrix products, arithmetic and copies ran while one was open for 8% -> 8% of each run, Pallas kernels for 0% -> 0%
where the time goes in v4:
time: 79.7 us; the launch traced here: 79.2 us
  Pallas kernels  55.1 us (69%)
  local copies, waits for them, and re-layouts  9.86 us (12%)
  other arithmetic  7.21 us (9%)
  starting transfers between devices  6.29 us (8%)
    pallas_call x1, Pallas kernels, all_sum_and_backward(): pl.pallas_call(functools.partial(reduce_kernel, space_size, rep_size), ou...  41.1 us
    pallas_call x1, Pallas kernels, run_forward(): pl.pallas_call(forward_kernel, out_shape=(jax.ShapeDtypeStruct((slots, ch...  14 us
    ppermute x1, starting transfers between devices, exchange_planes(): from_left = lax.ppermute(high, 'space', up)  5 us
    unnamed x10, local copies, waits for them, and re-layouts  1.88 us
  transfers between devices with their start and end apart: 2, of which 0 were waited for; matrix products, arithmetic and copies ran while one was open for 8% of the time, Pallas kernels for 0%

profile of v4, /device:TPU:1, one launch (start us, length us, event | category | flops | bytes accessed | tf_op | source)
XLA Modules:
  0.0 79.2 jit_solution(10404182344458534063)
XLA Ops:
  0.6 0.0 copy-start
  0.6 0.8 fusion.9
  1.4 1.0 %bitcast_multiply_fusion = bf16[4,64,512]{2,1,0:T(8,128)(2,1)S(1)} fusion(bf16[1,4,64,512]{3,2,1,0:T(8,128)(2,1)} %param.7, bf16[4,512]{1,0:T(4,128)(2,1)S(1)} %get-tuple-element.19), kind=kLoop, calls=%fused_computation.15 | loop fusion | flops 131072 | bytes 528384 | tf_op jit(solution)/shard_map/mul | solution.py:332
  2.4 0.0 copy-start.3
  2.4 0.1 fusion.8
  2.5 1.3 %collective-permute-start.1 = (bf16[4,64,64]{2,1,0:T(8,128)(2,1)S(1)}, bf16[4,64,64]{2,1,0:T(8,128)(2,1)S(1)}, u32[]{:S(2)}, u32[]{:S(2)}) collective-permute-start(bf16[4,64,64]{2,1,0:T(8,128)(2,1)S(1)} %get-tuple-element.17), channel_id=1, source_target_pairs={{8,0},{16,8},{24,16},{32,24},{40,32},{48,40},{56,48},{64,56},{72,6... | collective-permute-start | bytes 98312 | tf_op jit(solution)/shard_map/ppermute | solution.py:128
  3.8 5.0 %collective-permute-start = (bf16[4,64,64]{2,1,0:T(8,128)(2,1)S(1)}, bf16[4,64,64]{2,1,0:T(8,128)(2,1)S(1)}, u32[]{:S(2)}, u32[]{:S(2)}) collective-permute-start(bf16[4,64,64]{2,1,0:T(8,128)(2,1)S(1)} %get-tuple-element.16), channel_id=1, source_target_pairs={{0,8},{8,16},{16,24},{24,32},{32,40},{40,48},{48,56},{56,64},{64,7... | collective-permute-start | bytes 98312 | tf_op jit(solution)/shard_map/ppermute | solution.py:127
  8.8 0.8 squeeze.10
  9.6 0.7 add.24
  10.2 0.1 add.25
  10.3 0.7 add_multiply_fusion
  11.0 0.1 sub.12
  11.1 0.5 compare_select_fusion.tbl_ref
  11.6 0.6 copy.23
  12.2 0.0 copy-done
  12.2 0.3 copy.16
  12.5 1.1 %reshape.67.w_ref = bf16[64,1728]{1,0:T(8,128)(2,1)} reshape(bf16[64,27,64]{2,1,0:T(8,128)(2,1)S(1)} %copy.16) | data formatting | bytes 442368 | tf_op jit(solution)/shard_map/reshape | solution.py:335
  13.6 0.0 copy-done.3
  13.6 0.7 copy.17.bias_ref
  14.3 0.9 %copy.20.wt_ref = bf16[64,1728]{1,0:T(8,128)(2,1)} copy(bf16[64,1728]{0,1:T(8,128)(2,1)S(1)} %bitcast.22) | data formatting | bytes 442368 | tf_op jit(solution)/shard_map/reshape | solution.py:336
  15.2 0.1 pad.20.clone
  15.2 0.0 collective-permute-done.1
  15.3 0.0 collective-permute-done
  15.3 1.1 %fusion.5.x_ref = bf16[13,64,512]{2,1,0:T(8,128)(2,1)} fusion(bf16[4,64,64]{2,1,0:T(8,128)(2,1)S(1)} %collective-permute-done.1, bf16[4,64,64]{2,1,0:T(8,128)(2,1)S(1)} %collective-permute-done, bf16[4,64,512]{2,1,0:T(8,128)(2,1)S(1)} %bitcast_multiply_fusion, bf16[13]{0:T(256)(128)(2,1)S(1)} %pad.20.clone), kind=kLoop, calls=%fused_computation.9 | loop fusion | flops 6815744 | bytes 1179674 | tf_op jit(solution)/shard_map/concatenate | solution.py:132
  16.3 14.0 %shard_map.102 = (bf16[4,64,512]{2,1,0:T(8,128)(2,1)}, bf16[4,64,512]{2,1,0:T(8,128)(2,1)}, f32[64,1728]{1,0:T(8,128)}, f32[64,1]{1,0:T(8,128)}) custom-call(s32[104]{0:T(128)} %compare_select_fusion.tbl_ref, bf16[13,64,512]{2,1,0:T(8,128)(2,1)} %fusion.5.x_ref, bf16[4,64,512]{2,1,0:T(8,128)(2,1)} %bitcast.23, f32[4,1,512]{2,1,0:T(1,128)} %bitcast.27, ...), custom_call_target="tpu_custom_call" | custom-call | tf_op jit(solution)/shard_map/pallas_call | solution.py:105
  30.3 1.4 %reshape.69 = f32[64,27,64]{2,1,0:T(8,128)S(1)} reshape(f32[64,1728]{1,0:T(8,128)} %get-tuple-element.11) | data formatting | bytes 884736 | tf_op jit(solution)/shard_map/reshape | solution.py:340
  31.7 0.5 copy.18
  32.3 0.0 copy-start.2
  32.3 0.2 reshape.70
  32.5 0.6 copy-done.2
  33.0 0.1 reduce
  33.1 0.8 %fusion.7.x_ref = f32[1024,128]{1,0:T(8,128)} fusion(f32[64]{0:T(128)S(1)} %reduce, f32[110592]{0:T(1024)S(1)} %reshape.70), kind=kLoop, calls=%fused_computation.12 | loop fusion | flops 524288 | bytes 966912 | tf_op jit(solution)/shard_map/reshape | solution.py:292
  34.0 41.1 %shard_map.103 = (f32[1024,128]{1,0:T(8,128)}, bf16[4,64,512]{2,1,0:T(8,128)(2,1)}) custom-call(s32[104]{0:T(128)} %compare_select_fusion.tbl_ref, f32[1024,128]{1,0:T(8,128)} %fusion.7.x_ref, bf16[4,64,512]{2,1,0:T(8,128)(2,1)} %get-tuple-element.13.gp_ref, bf16[4,64,512]{2,1,0:T(8,128)(2,1)} %bitcast.24, f32[4,1,512]{2,1,0:T(1,128)} %bitcast.28, ...), custom_call_target="tpu_custom_call" | custom-call | tf_op jit(solution)/shard_map/pallas_call | solution.py:300
  75.1 0.0 copy-start.1
  75.1 1.1 %slice_multiply_fusion = f32[864,128]{1,0:T(8,128)S(1)} fusion(f32[1024,128]{1,0:T(8,128)} %get-tuple-element.15), kind=kLoop, calls=%fused_computation.14 | loop fusion | flops 110592 | bytes 884736 | tf_op jit(solution)/shard_map/mul | solution.py:347
  76.2 1.1 %mul.32 = f32[27,64,64]{2,1,0:T(8,128)} reshape(f32[864,128]{1,0:T(8,128)S(1)} %slice_multiply_fusion) | data formatting | bytes 884736 | tf_op jit(solution)/shard_map/mul | solution.py:347
  77.3 1.2 %slice_multiply_fusion.1 = f32[64]{0:T(128)} fusion(f32[131072]{0:T(1024)} %bitcast.25), kind=kLoop, calls=%fused_computation.19 | loop fusion | flops 64 | bytes 512 | tf_op jit(solution)/shard_map/mul | solution.py:347
  78.5 0.0 copy-done.1
  78.5 0.7 copy.25
  (1 shorter events, 0.0 us)
Async XLA Ops:
  0.6 11.6 %copy-start = (bf16[27,64,64]{2,1,0:T(8,128)(2,1)S(1)}, bf16[27,64,64]{2,1,0:T(8,128)(2,1)}, u32[]{:S(2)}) copy-start(bf16[27,64,64]{2,1,0:T(8,128)(2,1)} %param.9) | copy-start | bytes 663556
  2.4 11.2 %copy-start.3 = (f32[64]{0:T(128)S(1)}, f32[64]{0:T(128)}, u32[]{:S(2)}) copy-start(f32[64]{0:T(128)} %param.10) | copy-start | bytes 772
  2.5 12.8 %collective-permute-start.1 = (bf16[4,64,64]{2,1,0:T(8,128)(2,1)S(1)}, bf16[4,64,64]{2,1,0:T(8,128)(2,1)S(1)}, u32[]{:S(2)}, u32[]{:S(2)}) collective-permute-start(bf16[4,64,64]{2,1,0:T(8,128)(2,1)S(1)} %get-tuple-element.17), channel_id=1, source_target_pairs={{8,0},{16,8},{24,16},{32,24},{40,32},{48,40},{56,48},{64,56},{72,6... | collective-permute-start | bytes 98312 | tf_op jit(solution)/shard_map/ppermute | solution.py:128
  3.8 11.5 %collective-permute-start = (bf16[4,64,64]{2,1,0:T(8,128)(2,1)S(1)}, bf16[4,64,64]{2,1,0:T(8,128)(2,1)S(1)}, u32[]{:S(2)}, u32[]{:S(2)}) collective-permute-start(bf16[4,64,64]{2,1,0:T(8,128)(2,1)S(1)} %get-tuple-element.16), channel_id=1, source_target_pairs={{0,8},{8,16},{16,24},{24,32},{32,40},{40,48},{48,56},{56,64},{64,7... | collective-permute-start | bytes 98312 | tf_op jit(solution)/shard_map/ppermute | solution.py:127
  32.3 0.8 copy-start.2
  75.1 3.4 %copy-start.1 = (bf16[4,64,512]{2,1,0:T(8,128)(2,1)S(1)}, bf16[4,64,512]{2,1,0:T(8,128)(2,1)}, u32[]{:S(2)}) copy-start(bf16[4,64,512]{2,1,0:T(8,128)(2,1)} %get-tuple-element.14) | copy-start | bytes 786436

commit v5 on v4

--- a/solution.py
+++ b/solution.py
@@ -65,9 +65,38 @@
     return edges
 
 
-def forward_kernel(tbl_ref, x_ref, cot_ref, occ_ref, w_ref, bias_ref, out_ref, gp_ref, dw_ref, db_ref, col_ref):
+def forward_kernel(
+    space_size, tbl_ref, xm_ref, cot_ref, occ_ref, w_ref, bias_ref, out_ref, gp_ref, dw_ref, db_ref,
+    col_ref, x_ref, plane_send, plane_recv,
+):
     slots, channels, voxels = cot_ref.shape
     edges = edge_masks((1, voxels))
+    space_i = lax.axis_index("space")
+    rep_i = lax.axis_index("rep")
+    mesh_ids = pl.DeviceIdType.MESH
+    sides = ((space_i + 1) % space_size, (space_i + space_size - 1) % space_size)
+    x_ref[pl.ds(slots, 2 * slots + 1)] = jnp.zeros((2 * slots + 1, channels, voxels), x_ref.dtype)
+    x_ref[pl.ds(0, slots)] = xm_ref[...]
+    barrier = pltpu.get_barrier_semaphore()
+    for side in sides:
+        pl.semaphore_signal(barrier, 1, device_id=(side, rep_i), device_id_type=mesh_ids)
+    pl.semaphore_wait(barrier, 2)
+    planes = []
+    for way, side in enumerate(sides):
+        lanes = pl.ds(voxels - 128, 128) if way == 0 else pl.ds(0, 128)
+        for brick in range(slots):
+            copy = pltpu.make_async_remote_copy(
+                src_ref=xm_ref.at[brick, :, lanes],
+                dst_ref=x_ref.at[(way + 1) * slots + brick, :, lanes],
+                send_sem=plane_send.at[way, brick],
+                recv_sem=plane_recv.at[way, brick],
+                device_id=(side, rep_i),
+                device_id_type=mesh_ids,
+            )
+            copy.start()
+            planes.append(copy)
+    for copy in planes:
+        copy.wait()
     dw_ref[...] = jnp.zeros_like(dw_ref)
     db_ref[...] = jnp.zeros_like(db_ref)
 
@@ -100,10 +129,10 @@
     return [pl.BlockSpec(memory_space=pltpu.VMEM)] * n
 
 
-def run_forward(tbl, table, cot, occ, w_all, bias):
+def run_forward(tbl, masked, cot, occ, w_all, bias):
     slots, channels, voxels = cot.shape
     return pl.pallas_call(
-        forward_kernel,
+        functools.partial(forward_kernel, lax.axis_size("space")),
         out_shape=(
             jax.ShapeDtypeStruct((slots, channels, voxels), jnp.bfloat16),
             jax.ShapeDtypeStruct((slots, channels, voxels), jnp.bfloat16),
@@ -112,9 +141,15 @@
         ),
         in_specs=[pl.BlockSpec(memory_space=pltpu.SMEM)] + vmem_specs(5),
         out_specs=tuple(vmem_specs(4)),
-        scratch_shapes=[pltpu.VMEM((27 * channels, voxels), jnp.bfloat16)],
-        interpret=INTERPRET,
-    )(tbl, table, cot, occ, w_all, bias)
+        scratch_shapes=[
+            pltpu.VMEM((27 * channels, voxels), jnp.bfloat16),
+            pltpu.VMEM((3 * slots + 1, channels, voxels), jnp.bfloat16),
+            pltpu.SemaphoreType.DMA((2, slots)),
+            pltpu.SemaphoreType.DMA((2, slots)),
+        ],
+        compiler_params=pltpu.CompilerParams(collective_id=1, has_side_effects=True),
+        interpret=REMOTE_INTERPRET,
+    )(tbl, masked, cot, occ, w_all, bias)
 
 
 def exchange_planes(field):
@@ -335,7 +370,7 @@
     w_all = weight.transpose(1, 0, 2).reshape(channels, 27 * channels)
     w_t = weight.transpose(2, 0, 1).reshape(channels, 27 * channels)
     result, grad_pre, dw, db = run_forward(
-        tbl, exchange_planes(masked), incoming, keep_float, w_all, bias.reshape(channels, 1)
+        tbl, masked, incoming, keep_float, w_all, bias.reshape(channels, 1)
     )
     weight_terms = dw.reshape(channels, 27, channels).transpose(1, 0, 2)
     weight_total, bias_total, in_grad = all_sum_and_backward(

time: 79.7 us -> 78.3 us (0.982)
  starting transfers between devices: 6.29 us -> 0 us
  Pallas kernels: 55.1 us -> 60.8 us
  other arithmetic: 7.21 us -> 6.14 us
    pallas_call x1, Pallas kernels: 14 us -> 25 us  [run_forward(): pl.pallas_call(functools.partial(forward_kernel, lax.axis_size('space')),...]
    ppermute x2 -> x0, starting transfers between devices: 6.29 us -> none  [the longest x1 5 us: exchange_planes(): from_left = lax.ppermute(high, 'space', up)]
    pallas_call x1, Pallas kernels: 41.1 us -> 35.8 us  [all_sum_and_backward(): pl.pallas_call(functools.partial(reduce_kernel, space_size, rep_size), ou...]
    unnamed x10 -> x17, local copies, waits for them, and re-layouts: 1.88 us -> 3.03 us
    concatenate x1 -> x0, other arithmetic: 1.05 us -> none  [exchange_planes(): return jnp.concatenate([field, left, right, zero])]
  transfers between devices with their start and end apart: 2 -> 0, of which waited for: 0 -> 0; matrix products, arithmetic and copies ran while one was open for 8% -> 0% of each run, Pallas kernels for 0% -> 0%
where the time goes in v5:
time: 78.3 us; the launch traced here: 77.9 us
  Pallas kernels  60.8 us (78%)
  local copies, waits for them, and re-layouts  10.3 us (13%)
  other arithmetic  6.14 us (8%)
    pallas_call x1, Pallas kernels, all_sum_and_backward(): pl.pallas_call(functools.partial(reduce_kernel, space_size, rep_size), ou...  35.8 us
    pallas_call x1, Pallas kernels, run_forward(): pl.pallas_call(functools.partial(forward_kernel, lax.axis_size('space')),...  25 us
    unnamed x17, local copies, waits for them, and re-layouts  3.03 us
    mul x1, other arithmetic, on_device(): masked = feats[0] * filled.astype(jnp.bfloat16)[:, None, :]  1.67 us

profile of v5, /device:TPU:1, one launch (start us, length us, event | category | flops | bytes accessed | tf_op | source)
XLA Modules:
  0.0 77.9 jit_solution(11970692348937972951)
XLA Ops:
  0.6 0.0 copy-start.6
  0.6 0.0 copy-start.5
  0.7 0.0 copy-start.3
  0.7 0.0 copy-start
  0.7 0.8 %squeeze.10 = s32[104]{0:T(128)S(1)} reshape(s32[1,4,26]{2,1,0:T(4,128)} %param.11) | data formatting | bytes 832 | tf_op jit(solution)/shard_map/squeeze | solution.py:369
  1.5 0.0 copy-done.5
  1.5 0.1 add.21
  1.6 0.0 copy-done.6
  1.6 0.1 sub.12
  1.7 0.5 compare_select_fusion.tbl_ref
  2.2 0.0 copy-done.3
  2.2 1.7 %bitcast_multiply_fusion.xm_ref = bf16[4,64,512]{2,1,0:T(8,128)(2,1)} fusion(bf16[1,4,64,512]{3,2,1,0:T(8,128)(2,1)} %param.7, bf16[4,512]{1,0:T(4,128)(2,1)S(1)} %get-tuple-element.17), kind=kLoop, calls=%fused_computation.4 | loop fusion | flops 131072 | bytes 528384 | tf_op jit(solution)/shard_map/mul | solution.py:367
  3.9 0.6 copy.23
  4.5 0.0 copy-done
  4.5 0.3 copy.16
  4.8 1.1 %reshape.67.w_ref = bf16[64,1728]{1,0:T(8,128)(2,1)} reshape(bf16[64,27,64]{2,1,0:T(8,128)(2,1)S(1)} %copy.16) | data formatting | bytes 442368 | tf_op jit(solution)/shard_map/reshape | solution.py:370
  5.9 0.0 copy-start.4
  5.9 0.7 copy-done.4
  6.6 0.7 copy.17.bias_ref
  7.3 25.0 %shard_map.102 = (bf16[4,64,512]{2,1,0:T(8,128)(2,1)}, bf16[4,64,512]{2,1,0:T(8,128)(2,1)}, f32[64,1728]{1,0:T(8,128)}, f32[64,1]{1,0:T(8,128)}) custom-call(s32[104]{0:T(128)} %compare_select_fusion.tbl_ref, bf16[4,64,512]{2,1,0:T(8,128)(2,1)} %bitcast_multiply_fusion.xm_ref, bf16[4,64,512]{2,1,0:T(8,128)(2,1)} %bitcast.22, f32[4,1,512]{2,1,0:T(1,128)} %bitcast.27, ...), custom_call_target="tpu_custom_call" | custom-call | tf_op jit(solution)/shard_map/pallas_call | solution.py:134
  32.2 0.9 %reduce = f32[64]{0:T(128)S(1)} reduce(f32[64,1]{1,0:T(8,128)} %get-tuple-element.12, f32[]{:T(128)} %constant.37), dimensions={1}, to_apply=%get-tuple-element.12.reduce_sub_computation | reduce | bytes 516 | tf_op jit(solution)/shard_map/pallas_call | solution.py:134
  33.1 1.4 %reshape.69 = f32[64,27,64]{2,1,0:T(8,128)S(1)} reshape(f32[64,1728]{1,0:T(8,128)} %get-tuple-element.11) | data formatting | bytes 884736 | tf_op jit(solution)/shard_map/reshape | solution.py:375
  34.6 0.5 copy.18
  35.1 0.2 reshape.70
  35.3 0.8 %fusion.x_ref = f32[1024,128]{1,0:T(8,128)} fusion(f32[64]{0:T(128)S(1)} %reduce, f32[110592]{0:T(1024)S(1)} %reshape.70), kind=kLoop, calls=%fused_computation.1 | loop fusion | flops 524288 | bytes 966912 | tf_op jit(solution)/shard_map/reshape | solution.py:327
  36.1 0.9 %copy.20.wt_ref = bf16[64,1728]{1,0:T(8,128)(2,1)} copy(bf16[64,1728]{0,1:T(8,128)(2,1)S(1)} %bitcast.21) | data formatting | bytes 442368 | tf_op jit(solution)/shard_map/reshape | solution.py:371
  37.0 35.8 %shard_map.103 = (f32[1024,128]{1,0:T(8,128)}, bf16[4,64,512]{2,1,0:T(8,128)(2,1)}) custom-call(s32[104]{0:T(128)} %compare_select_fusion.tbl_ref, f32[1024,128]{1,0:T(8,128)} %fusion.x_ref, bf16[4,64,512]{2,1,0:T(8,128)(2,1)} %get-tuple-element.13.gp_ref, bf16[4,64,512]{2,1,0:T(8,128)(2,1)} %bitcast.23, f32[4,1,512]{2,1,0:T(1,128)} %bitcast.28, ...), custom_call_target="tpu_custom_call" | custom-call | tf_op jit(solution)/shard_map/pallas_call | solution.py:335
  72.8 1.1 %slice_multiply_fusion = f32[864,128]{1,0:T(8,128)S(1)} fusion(f32[1024,128]{1,0:T(8,128)} %get-tuple-element.15), kind=kLoop, calls=%fused_computation.3 | loop fusion | flops 110592 | bytes 884736 | tf_op jit(solution)/shard_map/mul | solution.py:382
  73.9 0.0 copy-start.1
  73.9 1.1 %mul.32 = f32[27,64,64]{2,1,0:T(8,128)} reshape(f32[864,128]{1,0:T(8,128)S(1)} %slice_multiply_fusion) | data formatting | bytes 884736 | tf_op jit(solution)/shard_map/mul | solution.py:382
  75.0 1.2 %slice_multiply_fusion.1 = f32[64]{0:T(128)} fusion(f32[131072]{0:T(1024)} %bitcast.24), kind=kLoop, calls=%fused_computation.8 | loop fusion | flops 64 | bytes 512 | tf_op jit(solution)/shard_map/mul | solution.py:382
  76.2 0.0 copy-done.1
  76.2 0.0 copy-start.2
  76.2 0.7 copy.26
  76.9 0.3 copy-done.2
  77.2 0.7 copy.27
  (4 shorter events, 0.0 us)
Async XLA Ops:
  0.6 1.0 %copy-start.6 = (s32[26]{0:T(128)S(1)}, s32[26]{0:T(128)}, u32[]{:S(2)}) copy-start(s32[26]{0:T(128)} %constant.26.clone) | copy-start | bytes 316
  0.6 0.9 %copy-start.5 = (s32[26]{0:T(128)S(1)}, s32[26]{0:T(128)}, u32[]{:S(2)}) copy-start(s32[26]{0:T(128)} %constant.36) | copy-start | bytes 316
  0.7 1.6 %copy-start.3 = (s32[1,4,512]{2,1,0:T(4,128)S(1)}, s32[1,4,512]{2,1,0:T(4,128)}, u32[]{:S(2)}) copy-start(s32[1,4,512]{2,1,0:T(4,128)} %param.12) | copy-start | bytes 24580
  0.7 3.8 %copy-start = (bf16[27,64,64]{2,1,0:T(8,128)(2,1)S(1)}, bf16[27,64,64]{2,1,0:T(8,128)(2,1)}, u32[]{:S(2)}) copy-start(bf16[27,64,64]{2,1,0:T(8,128)(2,1)} %param.9) | copy-start | bytes 663556
  5.9 0.7 copy-start.4
  73.9 2.3 %copy-start.1 = (bf16[4,64,512]{2,1,0:T(8,128)(2,1)S(1)}, bf16[4,64,512]{2,1,0:T(8,128)(2,1)}, u32[]{:S(2)}) copy-start(bf16[4,64,512]{2,1,0:T(8,128)(2,1)} %get-tuple-element.10) | copy-start | bytes 786436
  76.2 1.0 %copy-start.2 = (bf16[4,64,512]{2,1,0:T(8,128)(2,1)S(1)}, bf16[4,64,512]{2,1,0:T(8,128)(2,1)}, u32[]{:S(2)}) copy-start(bf16[4,64,512]{2,1,0:T(8,128)(2,1)} %get-tuple-element.14) | copy-start | bytes 786436

commit v6 on v5

--- a/solution.py
+++ b/solution.py
@@ -150,21 +150,6 @@
         compiler_params=pltpu.CompilerParams(collective_id=1, has_side_effects=True),
         interpret=REMOTE_INTERPRET,
     )(tbl, masked, cot, occ, w_all, bias)
-
-
-def exchange_planes(field):
-    size = lax.axis_size("space")
-    up = [(i, i + 1) for i in range(size - 1)]
-    down = [(i + 1, i) for i in range(size - 1)]
-    voxels = field.shape[-1]
-    low = field[:, :, :64]
-    high = field[:, :, voxels - 64 :]
-    from_left = lax.ppermute(high, "space", up)
-    from_right = lax.ppermute(low, "space", down)
-    left = jnp.pad(from_left, ((0, 0), (0, 0), (voxels - 64, 0)))
-    right = jnp.pad(from_right, ((0, 0), (0, 0), (0, voxels - 64)))
-    zero = jnp.zeros((1,) + field.shape[1:], field.dtype)
-    return jnp.concatenate([field, left, right, zero])
 
 
 def slot_table(neighbour_ids, my_index):
@@ -372,10 +357,10 @@
     result, grad_pre, dw, db = run_forward(
         tbl, masked, incoming, keep_float, w_all, bias.reshape(channels, 1)
     )
-    weight_terms = dw.reshape(channels, 27, channels).transpose(1, 0, 2)
     weight_total, bias_total, in_grad = all_sum_and_backward(
-        weight_terms, db.reshape(channels), tbl, grad_pre, incoming, keep_float, w_t
-    )
+        dw, db.reshape(channels), tbl, grad_pre, incoming, keep_float, w_t
+    )
+    weight_total = weight_total.reshape(channels, 27, channels).transpose(1, 0, 2)
     normaliser = 1.0 / math.sqrt(
         feats.shape[0] * lax.axis_size("rep") * slot_count * lax.axis_size("space") * 512
     )

time: 78.3 us -> 78.7 us (level)
  local copies, waits for them, and re-layouts: 10.3 us -> 11.5 us
  other arithmetic: 6.14 us -> 5.19 us
    unnamed x17 -> x22, local copies, waits for them, and re-layouts: 3.03 us -> 5.7 us
    reshape x1 -> x0, local copies, waits for them, and re-layouts: 1.44 us -> none  [on_device(): weight_terms = dw.reshape(channels, 27, channels).transpose(1, 0, 2)]
    reshape x1, local copies, waits for them, and re-layouts: 0.18 us -> 1.27 us  [all_sum_and_backward(): flat = jnp.concatenate([weight_terms.reshape(-1), bias_terms])]
    reshape x1, local copies, waits for them, and re-layouts: 0.89 us -> 1.95 us  [on_device(): w_t = weight.transpose(2, 0, 1).reshape(channels, 27 * channels)]
    mul x1, other arithmetic: 1.67 us -> 0.72 us  [on_device(): masked = feats[0] * filled.astype(jnp.bfloat16)[:, None, :]]
    mul x1, local copies, waits for them, and re-layouts: 1.12 us -> 0.24 us  [on_device(): weight_total * normaliser]
where the time goes in v6:
time: 78.7 us; the launch traced here: 78.2 us
  Pallas kernels  60.8 us (77%)
  local copies, waits for them, and re-layouts  11.5 us (15%)
  other arithmetic  5.19 us (7%)
    pallas_call x1, Pallas kernels, all_sum_and_backward(): pl.pallas_call(functools.partial(reduce_kernel, space_size, rep_size), ou...  35.8 us
    pallas_call x1, Pallas kernels, run_forward(): pl.pallas_call(functools.partial(forward_kernel, lax.axis_size('space')),...  25 us
    unnamed x22, local copies, waits for them, and re-layouts  5.7 us
    reshape x1, local copies, waits for them, and re-layouts, on_device(): w_t = weight.transpose(2, 0, 1).reshape(channels, 27 * channels)  1.95 us

profile of v6, /device:TPU:1, one launch (start us, length us, event | category | flops | bytes accessed | tf_op | source)
XLA Modules:
  0.0 78.2 jit_solution(8736663941127121339)
XLA Ops:
  0.6 0.0 copy-start.8
  0.6 0.0 copy-start.5
  0.7 0.6 copy-done.8
  1.3 0.0 copy-start.4
  1.3 0.0 copy-done.5
  1.3 0.1 squeeze.10
  1.4 0.0 copy-start.7
  1.4 0.1 sub.12
  1.5 0.6 copy-done.7
  2.1 0.1 add.21
  2.2 0.5 compare_select_fusion.tbl_ref
  2.7 0.0 copy-done.4
  2.7 0.6 copy.24
  3.3 0.0 copy-start.6
  3.3 0.7 copy-done.6
  4.0 0.0 copy-start.1
  4.0 0.7 copy.18.bias_ref
  4.7 0.0 copy-start
  4.7 1.9 %copy.21.wt_ref = bf16[64,1728]{1,0:T(8,128)(2,1)} copy(bf16[64,1728]{0,1:T(8,128)(2,1)} %bitcast.20) | data formatting | bytes 442368 | tf_op jit(solution)/shard_map/reshape | solution.py:356
  6.6 0.0 copy-done.1
  6.6 0.7 bitcast_multiply_fusion.xm_ref
  7.3 0.0 copy-done
  7.3 0.3 copy.17
  7.6 1.1 %reshape.62.w_ref = bf16[64,1728]{1,0:T(8,128)(2,1)} reshape(bf16[64,27,64]{2,1,0:T(8,128)(2,1)S(1)} %copy.17) | data formatting | bytes 442368 | tf_op jit(solution)/shard_map/reshape | solution.py:355
  8.8 25.0 %shard_map.102 = (bf16[4,64,512]{2,1,0:T(8,128)(2,1)}, bf16[4,64,512]{2,1,0:T(8,128)(2,1)}, f32[64,1728]{1,0:T(8,128)}, f32[64,1]{1,0:T(8,128)}) custom-call(s32[104]{0:T(128)} %compare_select_fusion.tbl_ref, bf16[4,64,512]{2,1,0:T(8,128)(2,1)} %bitcast_multiply_fusion.xm_ref, bf16[4,64,512]{2,1,0:T(8,128)(2,1)} %bitcast.22, f32[4,1,512]{2,1,0:T(1,128)} %bitcast.27, ...), custom_call_target="tpu_custom_call" | custom-call | tf_op jit(solution)/shard_map/pallas_call | solution.py:134
  33.7 0.9 %reduce = f32[64]{0:T(128)S(1)} reduce(f32[64,1]{1,0:T(8,128)} %get-tuple-element.12, f32[]{:T(128)} %constant.37), dimensions={1}, to_apply=%get-tuple-element.12.reduce_sub_computation | reduce | bytes 516 | tf_op jit(solution)/shard_map/pallas_call | solution.py:134
  34.6 1.3 %reshape.64 = f32[110592]{0:T(1024)S(1)} reshape(f32[64,1728]{1,0:T(8,128)} %get-tuple-element.11) | data formatting | bytes 884736 | tf_op jit(solution)/shard_map/reshape | solution.py:304
  35.9 0.8 %fusion.x_ref = f32[1024,128]{1,0:T(8,128)} fusion(f32[64]{0:T(128)S(1)} %reduce, f32[110592]{0:T(1024)S(1)} %reshape.64), kind=kLoop, calls=%fused_computation.1 | loop fusion | flops 524288 | bytes 966912 | tf_op jit(solution)/shard_map/reshape | solution.py:312
  36.7 35.8 %shard_map.103 = (f32[1024,128]{1,0:T(8,128)}, bf16[4,64,512]{2,1,0:T(8,128)(2,1)}) custom-call(s32[104]{0:T(128)} %compare_select_fusion.tbl_ref, f32[1024,128]{1,0:T(8,128)} %fusion.x_ref, bf16[4,64,512]{2,1,0:T(8,128)(2,1)} %get-tuple-element.13.gp_ref, bf16[4,64,512]{2,1,0:T(8,128)(2,1)} %bitcast.23, f32[4,1,512]{2,1,0:T(1,128)} %bitcast.28, ...), custom_call_target="tpu_custom_call" | custom-call | tf_op jit(solution)/shard_map/pallas_call | solution.py:320
  72.6 1.2 %slice_multiply_fusion.1 = f32[64]{0:T(128)} fusion(f32[131072]{0:T(1024)} %bitcast.24), kind=kLoop, calls=%fused_computation.8 | loop fusion | flops 64 | bytes 512 | tf_op jit(solution)/shard_map/mul | solution.py:367
  73.7 1.1 %slice_multiply_fusion = f32[864,128]{1,0:T(8,128)S(1)} fusion(f32[1024,128]{1,0:T(8,128)} %get-tuple-element.15), kind=kLoop, calls=%fused_computation.3 | loop fusion | flops 110592 | bytes 884736 | tf_op jit(solution)/shard_map/mul | solution.py:367
  74.8 0.2 mul.35
  75.0 0.0 copy-start.2
  75.1 1.4 %copy.20 = f32[27,64,64]{2,1,0:T(8,128)} copy(f32[27,64,64]{2,0,1:T(8,128)S(1)} %bitcast.19) | data formatting | bytes 884736
  76.5 0.0 copy-done.2
  76.5 0.0 copy-start.3
  76.5 0.7 copy.27
  77.2 0.3 copy-done.3
  77.5 0.7 copy.28
  (4 shorter events, 0.0 us)
Async XLA Ops:
  0.6 0.7 copy-start.8
  0.6 0.7 copy-start.5
  1.3 1.4 %copy-start.4 = (s32[1,4,512]{2,1,0:T(4,128)S(1)}, s32[1,4,512]{2,1,0:T(4,128)}, u32[]{:S(2)}) copy-start(s32[1,4,512]{2,1,0:T(4,128)} %param.12) | copy-start | bytes 24580
  1.4 0.7 copy-start.7
  3.3 0.7 copy-start.6
  4.0 2.7 %copy-start.1 = (bf16[1,4,64,512]{3,2,1,0:T(8,128)(2,1)S(1)}, bf16[1,4,64,512]{3,2,1,0:T(8,128)(2,1)}, u32[]{:S(2)}) copy-start(bf16[1,4,64,512]{3,2,1,0:T(8,128)(2,1)} %param.7) | copy-start | bytes 786436
  4.7 2.7 %copy-start = (bf16[27,64,64]{2,1,0:T(8,128)(2,1)S(1)}, bf16[27,64,64]{2,1,0:T(8,128)(2,1)}, u32[]{:S(2)}) copy-start(bf16[27,64,64]{2,1,0:T(8,128)(2,1)} %param.9) | copy-start | bytes 663556
  75.0 1.4 %copy-start.2 = (bf16[4,64,512]{2,1,0:T(8,128)(2,1)S(1)}, bf16[4,64,512]{2,1,0:T(8,128)(2,1)}, u32[]{:S(2)}) copy-start(bf16[4,64,512]{2,1,0:T(8,128)(2,1)} %get-tuple-element.10) | copy-start | bytes 786436
  76.5 1.0 %copy-start.3 = (bf16[4,64,512]{2,1,0:T(8,128)(2,1)S(1)}, bf16[4,64,512]{2,1,0:T(8,128)(2,1)}, u32[]{:S(2)}) copy-start(bf16[4,64,512]{2,1,0:T(8,128)(2,1)} %get-tuple-element.14) | copy-start | bytes 786436

commit v7 on v5

--- a/solution.py
+++ b/solution.py
@@ -195,7 +195,8 @@
 
 
 def reduce_kernel(
-    space_size, rep_size, tbl_ref, x_ref, gp_ref, cot_ref, occ_ref, wt_ref, o_ref, in_grad_ref, *scratch,
+    space_size, rep_size, weight_rows, scale, tbl_ref, x_ref, gp_ref, cot_ref, occ_ref, wt_ref,
+    o_ref, bias_out_ref, in_grad_ref, *scratch,
 ):
     levels = sum_levels(space_size, rep_size)
     count = len(levels)
@@ -312,10 +313,11 @@
             copy.wait()
         lo = pl.multiple_of(lo - r * length, 8)
         length = n * length
-    o_ref[...] = full[...]
-
-
-def all_sum_and_backward(weight_terms, bias_terms, tbl, grad_pre, incoming, keep_float, w_t):
+    o_ref[...] = full[pl.ds(0, weight_rows)] * scale
+    bias_out_ref[...] = full[pl.ds(weight_rows, 8)] * scale
+
+
+def all_sum_and_backward(weight_terms, bias_terms, tbl, grad_pre, incoming, keep_float, w_t, scale):
     flat = jnp.concatenate([weight_terms.reshape(-1), bias_terms])
     space_size = lax.axis_size("space")
     rep_size = lax.axis_size("rep")
@@ -332,14 +334,16 @@
         recvs.append(pltpu.VMEM((n, length, 128), jnp.float32))
     recvs.append(pltpu.VMEM((sizes[-1], length, 128), jnp.float32))
     slots, channels, voxels = incoming.shape
-    summed, in_grad = pl.pallas_call(
-        functools.partial(reduce_kernel, space_size, rep_size),
+    weight_rows = weight_terms.size // 128
+    summed, bias_rows, in_grad = pl.pallas_call(
+        functools.partial(reduce_kernel, space_size, rep_size, weight_rows, scale),
         out_shape=(
-            jax.ShapeDtypeStruct((rows, 128), jnp.float32),
+            jax.ShapeDtypeStruct((weight_rows, 128), jnp.float32),
+            jax.ShapeDtypeStruct((8, 128), jnp.float32),
             jax.ShapeDtypeStruct((slots, channels, voxels), jnp.bfloat16),
         ),
         in_specs=[pl.BlockSpec(memory_space=pltpu.SMEM)] + vmem_specs(5),
-        out_specs=tuple(vmem_specs(2)),
+        out_specs=tuple(vmem_specs(3)),
         scratch_shapes=[
             pltpu.VMEM((rows, 128), jnp.float32),
             pltpu.VMEM((rows, 128), jnp.float32),
@@ -355,8 +359,7 @@
         compiler_params=pltpu.CompilerParams(collective_id=0, has_side_effects=True),
         interpret=REMOTE_INTERPRET,
     )(tbl, x, grad_pre, incoming, keep_float, w_t)
-    x = summed.reshape(-1)[:whole]
-    return x[: weight_terms.size].reshape(weight_terms.shape), x[weight_terms.size :], in_grad
+    return summed.reshape(weight_terms.shape), bias_rows[0, : bias_terms.size], in_grad
 
 
 def on_device(feats, cotangent, weight, bias, neighbours, occupancy):
@@ -373,13 +376,13 @@
         tbl, masked, incoming, keep_float, w_all, bias.reshape(channels, 1)
     )
     weight_terms = dw.reshape(channels, 27, channels).transpose(1, 0, 2)
-    weight_total, bias_total, in_grad = all_sum_and_backward(
-        weight_terms, db.reshape(channels), tbl, grad_pre, incoming, keep_float, w_t
-    )
     normaliser = 1.0 / math.sqrt(
         feats.shape[0] * lax.axis_size("rep") * slot_count * lax.axis_size("space") * 512
     )
-    return (result[None], in_grad[None], weight_total * normaliser, bias_total * normaliser)
+    weight_total, bias_total, in_grad = all_sum_and_backward(
+        weight_terms, db.reshape(channels), tbl, grad_pre, incoming, keep_float, w_t, normaliser
+    )
+    return (result[None], in_grad[None], weight_total, bias_total)
 
 
 def solution(mesh):

time: 78.3 us -> 78.3 us (level)
  other arithmetic: 6.14 us -> 3.9 us
  local copies, waits for them, and re-layouts: 10.3 us -> 12.5 us
    mul x2 -> x0, other arithmetic: 2.24 us -> none  [the longest x1 1.18 us: on_device(): bias_total * normaliser]
    reshape x0 -> x1, local copies, waits for them, and re-layouts: none -> 2.17 us  [all_sum_and_backward(): summed.reshape(weight_terms.shape)]
    squeeze x0 -> x1, local copies, waits for them, and re-layouts: none -> 1.18 us  [all_sum_and_backward(): bias_rows[0, :bias_terms.size]]
    mul x1 -> x0, local copies, waits for them, and re-layouts: 1.12 us -> none  [on_device(): weight_total * normaliser]
where the time goes in v7:
time: 78.3 us; the launch traced here: 78 us
  Pallas kernels  60.8 us (78%)
  local copies, waits for them, and re-layouts  12.5 us (16%)
  other arithmetic  3.9 us (5%)
    pallas_call x1, Pallas kernels, all_sum_and_backward(): pl.pallas_call(functools.partial(reduce_kernel, space_size, rep_size, wei...  35.8 us
    pallas_call x1, Pallas kernels, run_forward(): pl.pallas_call(functools.partial(forward_kernel, lax.axis_size('space')),...  25 us
    unnamed x17, local copies, waits for them, and re-layouts  3.03 us
    reshape x1, local copies, waits for them, and re-layouts, all_sum_and_backward(): summed.reshape(weight_terms.shape)  2.17 us
    mul x1, other arithmetic, on_device(): masked = feats[0] * filled.astype(jnp.bfloat16)[:, None, :]  1.67 us

profile of v7, /device:TPU:1, one launch (start us, length us, event | category | flops | bytes accessed | tf_op | source)
XLA Modules:
  0.0 78.0 jit_solution(14500996553448324083)
XLA Ops:
  0.6 0.0 copy-start.6
  0.6 0.0 copy-start.5
  0.7 0.0 copy-start.3
  0.7 0.0 copy-start
  0.7 0.8 %squeeze.13 = s32[104]{0:T(128)S(1)} reshape(s32[1,4,26]{2,1,0:T(4,128)} %param.11) | data formatting | bytes 832 | tf_op jit(solution)/shard_map/squeeze | solution.py:372
  1.5 0.0 copy-done.5
  1.5 0.1 add.21
  1.6 0.0 copy-done.6
  1.6 0.1 sub.12
  1.7 0.5 compare_select_fusion.tbl_ref
  2.2 0.0 copy-done.3
  2.2 1.7 %bitcast_multiply_fusion.xm_ref = bf16[4,64,512]{2,1,0:T(8,128)(2,1)} fusion(bf16[1,4,64,512]{3,2,1,0:T(8,128)(2,1)} %param.7, bf16[4,512]{1,0:T(4,128)(2,1)S(1)} %get-tuple-element.19), kind=kLoop, calls=%fused_computation.3 | loop fusion | flops 131072 | bytes 528384 | tf_op jit(solution)/shard_map/mul | solution.py:370
  3.9 0.6 copy.23
  4.5 0.0 copy-done
  4.5 0.3 copy.16
  4.8 1.1 %reshape.61.w_ref = bf16[64,1728]{1,0:T(8,128)(2,1)} reshape(bf16[64,27,64]{2,1,0:T(8,128)(2,1)S(1)} %copy.16) | data formatting | bytes 442368 | tf_op jit(solution)/shard_map/reshape | solution.py:373
  5.9 0.0 copy-start.4
  5.9 0.7 copy-done.4
  6.6 0.7 copy.17.bias_ref
  7.3 25.0 %shard_map.102 = (bf16[4,64,512]{2,1,0:T(8,128)(2,1)}, bf16[4,64,512]{2,1,0:T(8,128)(2,1)}, f32[64,1728]{1,0:T(8,128)}, f32[64,1]{1,0:T(8,128)}) custom-call(s32[104]{0:T(128)} %compare_select_fusion.tbl_ref, bf16[4,64,512]{2,1,0:T(8,128)(2,1)} %bitcast_multiply_fusion.xm_ref, bf16[4,64,512]{2,1,0:T(8,128)(2,1)} %bitcast.23, f32[4,1,512]{2,1,0:T(1,128)} %bitcast.27, ...), custom_call_target="tpu_custom_call" | custom-call | tf_op jit(solution)/shard_map/pallas_call | solution.py:134
  32.3 0.9 %reduce = f32[64]{0:T(128)S(1)} reduce(f32[64,1]{1,0:T(8,128)} %get-tuple-element.13, f32[]{:T(128)} %constant.34), dimensions={1}, to_apply=%get-tuple-element.13.reduce_sub_computation | reduce | bytes 516 | tf_op jit(solution)/shard_map/pallas_call | solution.py:134
  33.1 1.4 %reshape.63 = f32[64,27,64]{2,1,0:T(8,128)S(1)} reshape(f32[64,1728]{1,0:T(8,128)} %get-tuple-element.12) | data formatting | bytes 884736 | tf_op jit(solution)/shard_map/reshape | solution.py:378
  34.6 0.5 copy.18
  35.1 0.2 reshape.64
  35.3 0.8 %fusion.x_ref = f32[1024,128]{1,0:T(8,128)} fusion(f32[64]{0:T(128)S(1)} %reduce, f32[110592]{0:T(1024)S(1)} %reshape.64), kind=kLoop, calls=%fused_computation.1 | loop fusion | flops 524288 | bytes 966912 | tf_op jit(solution)/shard_map/reshape | solution.py:329
  36.1 0.9 %copy.20.wt_ref = bf16[64,1728]{1,0:T(8,128)(2,1)} copy(bf16[64,1728]{0,1:T(8,128)(2,1)S(1)} %bitcast.22) | data formatting | bytes 442368 | tf_op jit(solution)/shard_map/reshape | solution.py:374
  37.0 35.8 %shard_map.103 = (f32[864,128]{1,0:T(8,128)}, f32[8,128]{1,0:T(8,128)}, bf16[4,64,512]{2,1,0:T(8,128)(2,1)}) custom-call(s32[104]{0:T(128)} %compare_select_fusion.tbl_ref, f32[1024,128]{1,0:T(8,128)} %fusion.x_ref, bf16[4,64,512]{2,1,0:T(8,128)(2,1)} %get-tuple-element.14.gp_ref, bf16[4,64,512]{2,1,0:T(8,128)(2,1)} %bitcast.24, f32[4,1,512]{2,1,0:T(1,128)} %bitcast.28, ...), custom_call_target="tpu_custom_call" | custom-call | tf_op jit(solution)/shard_map/pallas_call | solution.py:338
  72.8 0.0 copy-start.1
  72.9 2.2 %reshape.68 = f32[27,64,64]{2,1,0:T(8,128)} reshape(f32[864,128]{1,0:T(8,128)} %get-tuple-element.16) | data formatting | bytes 884736 | tf_op jit(solution)/shard_map/reshape | solution.py:362
  75.0 1.2 %slice_bitcast_fusion = f32[64]{0:T(128)} fusion(f32[8,128]{1,0:T(8,128)} %get-tuple-element.17), kind=kLoop, calls=%fused_computation.7 | loop fusion | bytes 512 | tf_op jit(solution)/shard_map/squeeze | solution.py:362
  76.2 0.0 copy-done.1
  76.2 0.0 copy-start.2
  76.2 0.7 copy.26
  76.9 0.3 copy-done.2
  77.3 0.7 copy.27
  (4 shorter events, 0.0 us)
Async XLA Ops:
  0.6 1.0 %copy-start.6 = (s32[26]{0:T(128)S(1)}, s32[26]{0:T(128)}, u32[]{:S(2)}) copy-start(s32[26]{0:T(128)} %constant.23.clone) | copy-start | bytes 316
  0.6 0.9 %copy-start.5 = (s32[26]{0:T(128)S(1)}, s32[26]{0:T(128)}, u32[]{:S(2)}) copy-start(s32[26]{0:T(128)} %constant.33) | copy-start | bytes 316
  0.7 1.6 %copy-start.3 = (s32[1,4,512]{2,1,0:T(4,128)S(1)}, s32[1,4,512]{2,1,0:T(4,128)}, u32[]{:S(2)}) copy-start(s32[1,4,512]{2,1,0:T(4,128)} %param.12) | copy-start | bytes 24580
  0.7 3.8 %copy-start = (bf16[27,64,64]{2,1,0:T(8,128)(2,1)S(1)}, bf16[27,64,64]{2,1,0:T(8,128)(2,1)}, u32[]{:S(2)}) copy-start(bf16[27,64,64]{2,1,0:T(8,128)(2,1)} %param.9) | copy-start | bytes 663556
  5.9 0.7 copy-start.4
  72.8 3.4 %copy-start.1 = (bf16[4,64,512]{2,1,0:T(8,128)(2,1)S(1)}, bf16[4,64,512]{2,1,0:T(8,128)(2,1)}, u32[]{:S(2)}) copy-start(bf16[4,64,512]{2,1,0:T(8,128)(2,1)} %get-tuple-element.11) | copy-start | bytes 786436
  76.2 1.0 %copy-start.2 = (bf16[4,64,512]{2,1,0:T(8,128)(2,1)S(1)}, bf16[4,64,512]{2,1,0:T(8,128)(2,1)}, u32[]{:S(2)}) copy-start(bf16[4,64,512]{2,1,0:T(8,128)(2,1)} %get-tuple-element.15) | copy-start | bytes 786436

commit v8 on v7

--- a/solution.py
+++ b/solution.py
@@ -313,7 +313,12 @@
             copy.wait()
         lo = pl.multiple_of(lo - r * length, 8)
         length = n * length
-    o_ref[...] = full[pl.ds(0, weight_rows)] * scale
+    half = o_ref.shape[1] // 2
+    width = o_ref.shape[2]
+    for k in range(o_ref.shape[0]):
+        block = full[pl.ds(k * half, half)] * scale
+        o_ref[k, pl.ds(0, half, stride=2), :] = block[:, :width]
+        o_ref[k, pl.ds(1, half, stride=2), :] = block[:, width:]
     bias_out_ref[...] = full[pl.ds(weight_rows, 8)] * scale
 
 
@@ -338,7 +343,7 @@
     summed, bias_rows, in_grad = pl.pallas_call(
         functools.partial(reduce_kernel, space_size, rep_size, weight_rows, scale),
         out_shape=(
-            jax.ShapeDtypeStruct((weight_rows, 128), jnp.float32),
+            jax.ShapeDtypeStruct(weight_terms.shape, jnp.float32),
             jax.ShapeDtypeStruct((8, 128), jnp.float32),
             jax.ShapeDtypeStruct((slots, channels, voxels), jnp.bfloat16),
         ),
@@ -359,7 +364,7 @@
         compiler_params=pltpu.CompilerParams(collective_id=0, has_side_effects=True),
         interpret=REMOTE_INTERPRET,
     )(tbl, x, grad_pre, incoming, keep_float, w_t)
-    return summed.reshape(weight_terms.shape), bias_rows[0, : bias_terms.size], in_grad
+    return summed, bias_rows[0, : bias_terms.size], in_grad
 
 
 def on_device(feats, cotangent, weight, bias, neighbours, occupancy):

time: 78.3 us -> 78 us (level)
    reshape x1 -> x0, local copies, waits for them, and re-layouts: 2.17 us -> none  [all_sum_and_backward(): summed.reshape(weight_terms.shape)]
    unnamed x17 -> x18, local copies, waits for them, and re-layouts: 3.03 us -> 4.58 us
where the time goes in v8:
time: 78 us; the launch traced here: 77.7 us
  Pallas kernels  61.1 us (78%)
  local copies, waits for them, and re-layouts  12 us (15%)
  other arithmetic  3.9 us (5%)
    pallas_call x1, Pallas kernels, all_sum_and_backward(): pl.pallas_call(functools.partial(reduce_kernel, space_size, rep_size, wei...  36.1 us
    pallas_call x1, Pallas kernels, run_forward(): pl.pallas_call(functools.partial(forward_kernel, lax.axis_size('space')),...  25 us
    unnamed x18, local copies, waits for them, and re-layouts  4.58 us
    mul x1, other arithmetic, on_device(): masked = feats[0] * filled.astype(jnp.bfloat16)[:, None, :]  1.67 us

profile of v8, /device:TPU:1, one launch (start us, length us, event | category | flops | bytes accessed | tf_op | source)
XLA Modules:
  0.0 77.7 jit_solution(1882679817465919705)
XLA Ops:
  0.6 0.0 copy-start.6
  0.6 0.0 copy-start.5
  0.7 0.0 copy-start.3
  0.7 0.0 copy-start
  0.7 0.8 %squeeze.13 = s32[104]{0:T(128)S(1)} reshape(s32[1,4,26]{2,1,0:T(4,128)} %param.11) | data formatting | bytes 832 | tf_op jit(solution)/shard_map/squeeze | solution.py:377
  1.5 0.0 copy-done.5
  1.5 0.1 add.21
  1.6 0.0 copy-done.6
  1.6 0.1 sub.12
  1.7 0.5 compare_select_fusion.tbl_ref
  2.2 0.0 copy-done.3
  2.2 1.7 %bitcast_multiply_fusion.xm_ref = bf16[4,64,512]{2,1,0:T(8,128)(2,1)} fusion(bf16[1,4,64,512]{3,2,1,0:T(8,128)(2,1)} %param.7, bf16[4,512]{1,0:T(4,128)(2,1)S(1)} %get-tuple-element.19), kind=kLoop, calls=%fused_computation.3 | loop fusion | flops 131072 | bytes 528384 | tf_op jit(solution)/shard_map/mul | solution.py:375
  3.9 0.6 copy.23
  4.5 0.0 copy-done
  4.5 0.3 copy.16
  4.8 1.1 %reshape.58.w_ref = bf16[64,1728]{1,0:T(8,128)(2,1)} reshape(bf16[64,27,64]{2,1,0:T(8,128)(2,1)S(1)} %copy.16) | data formatting | bytes 442368 | tf_op jit(solution)/shard_map/reshape | solution.py:378
  5.9 0.0 copy-start.4
  5.9 0.7 copy-done.4
  6.6 0.7 copy.17.bias_ref
  7.3 25.0 %shard_map.102 = (bf16[4,64,512]{2,1,0:T(8,128)(2,1)}, bf16[4,64,512]{2,1,0:T(8,128)(2,1)}, f32[64,1728]{1,0:T(8,128)}, f32[64,1]{1,0:T(8,128)}) custom-call(s32[104]{0:T(128)} %compare_select_fusion.tbl_ref, bf16[4,64,512]{2,1,0:T(8,128)(2,1)} %bitcast_multiply_fusion.xm_ref, bf16[4,64,512]{2,1,0:T(8,128)(2,1)} %bitcast.23, f32[4,1,512]{2,1,0:T(1,128)} %bitcast.27, ...), custom_call_target="tpu_custom_call" | custom-call | tf_op jit(solution)/shard_map/pallas_call | solution.py:134
  32.2 0.9 %reduce = f32[64]{0:T(128)S(1)} reduce(f32[64,1]{1,0:T(8,128)} %get-tuple-element.13, f32[]{:T(128)} %constant.34), dimensions={1}, to_apply=%get-tuple-element.13.reduce_sub_computation | reduce | bytes 516 | tf_op jit(solution)/shard_map/pallas_call | solution.py:134
  33.1 1.4 %reshape.60 = f32[64,27,64]{2,1,0:T(8,128)S(1)} reshape(f32[64,1728]{1,0:T(8,128)} %get-tuple-element.12) | data formatting | bytes 884736 | tf_op jit(solution)/shard_map/reshape | solution.py:383
  34.6 0.5 copy.18
  35.1 0.2 reshape.61
  35.3 0.8 %fusion.x_ref = f32[1024,128]{1,0:T(8,128)} fusion(f32[64]{0:T(128)S(1)} %reduce, f32[110592]{0:T(1024)S(1)} %reshape.61), kind=kLoop, calls=%fused_computation.1 | loop fusion | flops 524288 | bytes 966912 | tf_op jit(solution)/shard_map/reshape | solution.py:334
  36.1 0.9 %copy.20.wt_ref = bf16[64,1728]{1,0:T(8,128)(2,1)} copy(bf16[64,1728]{0,1:T(8,128)(2,1)S(1)} %bitcast.22) | data formatting | bytes 442368 | tf_op jit(solution)/shard_map/reshape | solution.py:379
  37.0 0.0 copy-start.2
  37.0 36.1 %shard_map.103 = (f32[27,64,64]{2,1,0:T(8,128)}, f32[8,128]{1,0:T(8,128)}, bf16[4,64,512]{2,1,0:T(8,128)(2,1)}) custom-call(s32[104]{0:T(128)} %compare_select_fusion.tbl_ref, f32[1024,128]{1,0:T(8,128)} %fusion.x_ref, bf16[4,64,512]{2,1,0:T(8,128)(2,1)} %get-tuple-element.14.gp_ref, bf16[4,64,512]{2,1,0:T(8,128)(2,1)} %bitcast.24, f32[4,1,512]{2,1,0:T(1,128)} %bitcast.28, ...), custom_call_target="tpu_custom_call" | custom-call | tf_op jit(solution)/shard_map/pallas_call | solution.py:343
  73.1 0.0 copy-start.1
  73.1 1.3 %slice_bitcast_fusion = f32[64]{0:T(128)} fusion(f32[8,128]{1,0:T(8,128)} %get-tuple-element.17), kind=kLoop, calls=%fused_computation.7 | loop fusion | bytes 512 | tf_op jit(solution)/shard_map/squeeze | solution.py:367
  74.4 0.0 copy-done.2
  74.4 0.7 copy.27
  75.1 1.7 %copy.28 = bf16[1,4,64,512]{3,2,1,0:T(8,128)(2,1)} copy(bf16[1,4,64,512]{3,2,1,0:T(8,128)(2,1)} %bitcast.26) | data formatting | bytes 524288
  76.8 0.0 copy-done.1
  76.8 0.9 %copy.29 = f32[27,64,64]{2,1,0:T(8,128)} copy(f32[27,64,64]{2,1,0:T(8,128)S(1)} %copy-done.1) | data formatting | bytes 884736
  (4 shorter events, 0.0 us)
Async XLA Ops:
  0.6 1.0 %copy-start.6 = (s32[26]{0:T(128)S(1)}, s32[26]{0:T(128)}, u32[]{:S(2)}) copy-start(s32[26]{0:T(128)} %constant.23.clone) | copy-start | bytes 316
  0.6 0.9 %copy-start.5 = (s32[26]{0:T(128)S(1)}, s32[26]{0:T(128)}, u32[]{:S(2)}) copy-start(s32[26]{0:T(128)} %constant.33) | copy-start | bytes 316
  0.7 1.6 %copy-start.3 = (s32[1,4,512]{2,1,0:T(4,128)S(1)}, s32[1,4,512]{2,1,0:T(4,128)}, u32[]{:S(2)}) copy-start(s32[1,4,512]{2,1,0:T(4,128)} %param.12) | copy-start | bytes 24580
  0.7 3.8 %copy-start = (bf16[27,64,64]{2,1,0:T(8,128)(2,1)S(1)}, bf16[27,64,64]{2,1,0:T(8,128)(2,1)}, u32[]{:S(2)}) copy-start(bf16[27,64,64]{2,1,0:T(8,128)(2,1)} %param.9) | copy-start | bytes 663556
  5.9 0.7 copy-start.4
  37.0 37.4 %copy-start.2 = (bf16[4,64,512]{2,1,0:T(8,128)(2,1)S(1)}, bf16[4,64,512]{2,1,0:T(8,128)(2,1)}, u32[]{:S(2)}) copy-start(bf16[4,64,512]{2,1,0:T(8,128)(2,1)} %get-tuple-element.11) | copy-start | bytes 786436
  73.1 3.7 %copy-start.1 = (f32[27,64,64]{2,1,0:T(8,128)S(1)}, f32[27,64,64]{2,1,0:T(8,128)}, u32[]{:S(2)}) copy-start(f32[27,64,64]{2,1,0:T(8,128)} %get-tuple-element.26) | copy-start | bytes 1327108
